TPU v7x, 32 devices: a whole 2x2x4 slice. The times are simulated.
32 devices in a mesh: dp: 16 (over z, x, core), ctx: 2 (over y).
Axes of the slice: x: 2, y: 2, z: 4, core: 2. Of those that a mesh axis runs over, the one named last changes fastest.
Arguments:
- inputs: bfloat16 [16, 1024, 768], P('dp', 'ctx'), may hold values from -6 to 6
- cotangent: bfloat16 [16, 1024, 768], P('dp', 'ctx'), may hold values from -6 to 6
- query_weight: bfloat16 [768, 768], P(('dp', 'ctx')), may hold values from -0.649519 to 0.649519
- query_bias: bfloat16 [768], P(('dp', 'ctx')), may hold values from -3 to 3
- key_weight: bfloat16 [768, 768], P(('dp', 'ctx')), may hold values from -0.21875 to 0.21875
- value_weight: bfloat16 [768, 768], P(('dp', 'ctx')), may hold values from -0.21875 to 0.21875
- value_bias: bfloat16 [768], P(('dp', 'ctx')), may hold values from -2 to 2
- output_weight: bfloat16 [768, 768], P(('dp', 'ctx')), may hold values from -0.875 to 0.875
- output_bias: bfloat16 [768], P(('dp', 'ctx')), may hold values from -2 to 2
- first_gain: bfloat16 [768], P(('dp', 'ctx')), may hold values from 0.5 to 1.5
- first_shift: bfloat16 [768], P(('dp', 'ctx')), may hold values from -2 to 2
- inner_weight: bfloat16 [768, 3072], P(('dp', 'ctx')), may hold values from -0.21875 to 0.21875
- inner_bias: bfloat16 [3072], P(('dp', 'ctx')), may hold values from -2 to 2
- outer_weight: bfloat16 [3072, 768], P(('dp', 'ctx')), may hold values from -0.15625 to 0.15625
- outer_bias: bfloat16 [768], P(('dp', 'ctx')), may hold values from -2 to 2
- second_gain: bfloat16 [768], P(('dp', 'ctx')), may hold values from 0.5 to 1.5
- second_shift: bfloat16 [768], P(('dp', 'ctx')), may hold values from -2 to 2
- lengths: int32 [16], P('dp'), may hold values from 256 to 1024, as said below
- random_blocks: int32 [16, 16, 12, 3], P('dp'), may hold values from 0 to 15
- threshold: int32 [1], replicated, may hold values from 100 to 399
Outputs:
- output: bfloat16 [16, 1024, 768], P('dp', 'ctx')
- input_grad: float32 [16, 1024, 768], P('dp', 'ctx')
- query_weight_grad: float32 [768, 768], P(('dp', 'ctx'))
- query_bias_grad: float32 [768], P(('dp', 'ctx'))
- key_weight_grad: float32 [768, 768], P(('dp', 'ctx'))
- value_weight_grad: float32 [768, 768], P(('dp', 'ctx'))
- value_bias_grad: float32 [768], P(('dp', 'ctx'))
- output_weight_grad: float32 [768, 768], P(('dp', 'ctx'))
- output_bias_grad: float32 [768], P(('dp', 'ctx'))
- first_gain_grad: float32 [768], P(('dp', 'ctx'))
- first_shift_grad: float32 [768], P(('dp', 'ctx'))
- inner_weight_grad: float32 [768, 3072], P(('dp', 'ctx'))
- inner_bias_grad: float32 [3072], P(('dp', 'ctx'))
- outer_weight_grad: float32 [3072, 768], P(('dp', 'ctx'))
- outer_bias_grad: float32 [768], P(('dp', 'ctx'))
- second_gain_grad: float32 [768], P(('dp', 'ctx'))
- second_shift_grad: float32 [768], P(('dp', 'ctx'))
- query_weight_clipped: bfloat16 [768, 768], P(('dp', 'ctx'))
- query_bias_clipped: bfloat16 [768], P(('dp', 'ctx'))
- key_weight_clipped: bfloat16 [768, 768], P(('dp', 'ctx'))
- logit_maxima: float32 [12], replicated
Inputs may be any that keep to these rules, and one draw needn't show every extreme that they name: `lengths`: each sequence's valid tokens are its first ones; at least one sequence has all 1024 valid.
All inputs are finite; a program needn't handle non-finite values.
Results may differ from a plain program's by a relative error of at most 0.015.
The roundings to bfloat16 on the way count: a program that leaves them out, or rounds other values in their place, can miss the bound.
Values may be sent and summed in bfloat16 or wider, within the bound.
A program may use at most 256 MiB of HBM per device.

v0:
```python
import jax
import jax.numpy as jnp
from jax import lax
from jax.sharding import PartitionSpec as P

H = 12
HD = 64
BLK = 64
LEN = 1024
NB = 16


norm_eps = 1e-12
neg_large = -1e30


def layer_norm(row_values, gain_vector, shift_vector):
    centre = row_values - jnp.mean(row_values, axis=-1, keepdims=True)
    spread = jnp.mean(centre * centre, axis=-1, keepdims=True)
    return centre * lax.rsqrt(spread + norm_eps) * gain_vector + shift_vector


def gelu_exact(values):
    return jax.nn.gelu(values, approximate=False)


def matmul(former, latter):
    return jnp.dot(former, latter, preferred_element_type=jnp.float32)


def contract_rows(former, latter):
    return lax.dot_general(
        former, latter, (((0,), (0,)), ((), ())), preferred_element_type=jnp.float32
    )


def times_transposed(former, latter):
    return lax.dot_general(
        former, latter, (((1,), (1,)), ((), ())), preferred_element_type=jnp.float32
    )


def column_sums(values):
    return jnp.sum(values.astype(jnp.float32), axis=0)


def candidate_blocks(length, random_here, first_block):
    block_count = random_here.shape[0]
    block_ids = first_block + jnp.arange(block_count, dtype=jnp.int32)
    last_block = (length - 1) // BLK
    fixed_ids = jnp.stack(
        [
            jnp.zeros_like(block_ids),
            jnp.zeros_like(block_ids) + last_block,
            block_ids - 1,
            block_ids,
            block_ids + 1,
        ],
        axis=-1,
    )
    picked = jnp.concatenate(
        [jnp.broadcast_to(fixed_ids[:, None, :], (block_count, H, 5)), random_here], axis=-1
    )
    in_range = (picked >= 0) & (picked < NB) & (picked * BLK < length)
    width_count = picked.shape[-1]
    earlier = jnp.arange(width_count)[:, None] > jnp.arange(width_count)[None, :]
    repeated = jnp.any((picked[..., :, None] == picked[..., None, :]) & earlier, axis=-1)
    usable = in_range & jnp.logical_not(repeated)
    safe_ids = jnp.clip(picked, 0, NB - 1)
    key_mask = usable[..., None] & (
        safe_ids[..., None] * BLK + jnp.arange(BLK, dtype=jnp.int32) < length
    )
    return (safe_ids, key_mask)


def select_blocks(whole_rows, safe_ids):
    blocked = whole_rows.reshape(NB, BLK, H, HD).transpose(0, 2, 1, 3)
    head_ids = jnp.arange(H)[None, :, None]
    return blocked[safe_ids, head_ids]


def global_rows(length, first_block, block_count):
    last_block = (length - 1) // BLK
    local_last = jnp.clip(last_block - first_block, 0, block_count - 1)
    chosen = jnp.stack([jnp.zeros((), jnp.int32), local_last])
    global_flags = jnp.stack(
        [
            first_block == 0,
            (last_block >= first_block)
            & (last_block < first_block + block_count)
            & (last_block != 0),
        ]
    )
    place_map = (jnp.arange(block_count)[:, None] == chosen[None, :]) & global_flags[None, :]
    return (chosen, global_flags, place_map, jnp.any(place_map, axis=1))


def place_rows(place_map, dense_values):
    shape_tail = (1,) * (dense_values.ndim - 1)
    return jnp.sum(
        jnp.where(place_map.reshape(place_map.shape + shape_tail), dense_values[None], 0.0), axis=1
    )


def attend_piece(query_rows, keys_whole, values_whole, length, random_here, first_block):
    scale_factor = HD ** (-0.5)
    block_count = random_here.shape[0]
    query_blocks = query_rows.reshape(block_count, BLK, H, HD)
    safe_ids, key_mask = candidate_blocks(length, random_here, first_block)
    key_sel = select_blocks(keys_whole, safe_ids)
    value_sel = select_blocks(values_whole, safe_ids)
    raw_sparse = (
        jnp.einsum("iqhd,ihckd->ihqck", query_blocks, key_sel, preferred_element_type=jnp.float32)
        * scale_factor
    )
    sparse_mask = key_mask[:, :, None, :, :]
    masked = jnp.where(sparse_mask, raw_sparse, neg_large)
    positions = first_block * BLK + jnp.arange(block_count * BLK, dtype=jnp.int32).reshape(
        block_count, BLK
    )
    query_live = positions < length
    counted = sparse_mask & query_live[:, None, :, None, None]
    top_sparse = jnp.max(jnp.where(counted, raw_sparse, neg_large), axis=(0, 2, 3, 4))
    flat_scores = masked.reshape(block_count, H, BLK, -1)
    row_top = jnp.max(flat_scores, axis=-1, keepdims=True)
    exponent = jnp.exp(flat_scores - row_top)
    row_total = jnp.sum(exponent, axis=-1, keepdims=True)
    softmax_low = (exponent / row_total).astype(jnp.bfloat16).reshape(masked.shape)
    mixture_sparse = jnp.einsum(
        "ihqck,ihckd->iqhd", softmax_low, value_sel, preferred_element_type=jnp.float32
    )
    log_sparse = (row_top + jnp.log(row_total))[..., 0]
    chosen, global_flags, place_map, global_mask = global_rows(length, first_block, block_count)
    dense_queries = query_blocks[chosen]
    raw_dense = (
        jnp.einsum(
            "gqhd,khd->ghqk",
            dense_queries,
            keys_whole.reshape(LEN, H, HD),
            preferred_element_type=jnp.float32,
        )
        * scale_factor
    )
    key_live = jnp.arange(LEN, dtype=jnp.int32) < length
    masked_dense = jnp.where(key_live[None, None, None, :], raw_dense, neg_large)
    dense_live = query_live[chosen] & global_flags[:, None]
    top_dense = jnp.max(
        jnp.where(
            key_live[None, None, None, :] & dense_live[:, None, :, None], raw_dense, neg_large
        ),
        axis=(0, 2, 3),
    )
    dense_top = jnp.max(masked_dense, axis=-1, keepdims=True)
    dense_exp = jnp.exp(masked_dense - dense_top)
    dense_total = jnp.sum(dense_exp, axis=-1, keepdims=True)
    dense_low = (dense_exp / dense_total).astype(jnp.bfloat16)
    mixture_dense = jnp.einsum(
        "ghqk,khd->gqhd",
        dense_low,
        values_whole.reshape(LEN, H, HD),
        preferred_element_type=jnp.float32,
    )
    log_dense = (dense_top + jnp.log(dense_total))[..., 0]
    mixture = jnp.where(
        global_mask[:, None, None, None], place_rows(place_map, mixture_dense), mixture_sparse
    )
    log_total = jnp.where(global_mask[:, None, None], place_rows(place_map, log_dense), log_sparse)
    return (
        mixture.reshape(block_count * BLK, H * HD).astype(jnp.bfloat16),
        log_total,
        jnp.maximum(top_sparse, top_dense),
    )


def attend_back(
    query_rows, grad_rows, log_total, keys_whole, values_whole, length, random_here, first_block
):
    scale_factor = HD ** (-0.5)
    block_count = random_here.shape[0]
    query_blocks = query_rows.reshape(block_count, BLK, H, HD)
    grad_blocks = grad_rows.reshape(block_count, BLK, H, HD)
    chosen, global_flags, place_map, global_mask = global_rows(length, first_block, block_count)
    grad_sparse = jnp.where(
        global_mask[:, None, None, None], jnp.zeros_like(grad_blocks), grad_blocks
    )
    safe_ids, key_mask = candidate_blocks(length, random_here, first_block)
    key_sel = select_blocks(keys_whole, safe_ids)
    value_sel = select_blocks(values_whole, safe_ids)
    raw_sparse = (
        jnp.einsum("iqhd,ihckd->ihqck", query_blocks, key_sel, preferred_element_type=jnp.float32)
        * scale_factor
    )
    masked = jnp.where(key_mask[:, :, None, :, :], raw_sparse, neg_large)
    softmax_full = jnp.exp(masked - log_total[:, :, :, None, None])
    grad_soft = jnp.einsum(
        "iqhd,ihckd->ihqck", grad_sparse, value_sel, preferred_element_type=jnp.float32
    )
    inner_sum = jnp.sum(softmax_full * grad_soft, axis=(3, 4), keepdims=True)
    grad_scores = (softmax_full * (grad_soft - inner_sum)).astype(jnp.bfloat16)
    query_sparse = (
        jnp.einsum("ihqck,ihckd->iqhd", grad_scores, key_sel, preferred_element_type=jnp.float32)
        * scale_factor
    )
    key_sel_grad = (
        jnp.einsum(
            "ihqck,iqhd->ihckd", grad_scores, query_blocks, preferred_element_type=jnp.float32
        )
        * scale_factor
    )
    value_sel_grad = jnp.einsum(
        "ihqck,iqhd->ihckd",
        softmax_full.astype(jnp.bfloat16),
        grad_sparse,
        preferred_element_type=jnp.float32,
    )
    head_ids = jnp.arange(H)[None, :, None]
    key_blocks = jnp.zeros((NB, H, BLK, HD), jnp.float32).at[safe_ids, head_ids].add(key_sel_grad)
    value_blocks = (
        jnp.zeros((NB, H, BLK, HD), jnp.float32).at[safe_ids, head_ids].add(value_sel_grad)
    )
    key_heads = keys_whole.reshape(LEN, H, HD)
    value_heads = values_whole.reshape(LEN, H, HD)
    dense_queries = query_blocks[chosen]
    dense_grads = jnp.where(
        global_flags[:, None, None, None], grad_blocks[chosen], jnp.zeros_like(grad_blocks[chosen])
    )
    raw_dense = (
        jnp.einsum("gqhd,khd->ghqk", dense_queries, key_heads, preferred_element_type=jnp.float32)
        * scale_factor
    )
    key_live = jnp.arange(LEN, dtype=jnp.int32) < length
    masked_dense = jnp.where(key_live[None, None, None, :], raw_dense, neg_large)
    dense_soft = jnp.exp(jnp.minimum(masked_dense - log_total[chosen][..., None], 0.0))
    dense_dprob = jnp.einsum(
        "gqhd,khd->ghqk", dense_grads, value_heads, preferred_element_type=jnp.float32
    )
    dense_inner = jnp.sum(dense_soft * dense_dprob, axis=-1, keepdims=True)
    dense_scores = (dense_soft * (dense_dprob - dense_inner)).astype(jnp.bfloat16)
    query_dense = (
        jnp.einsum("ghqk,khd->gqhd", dense_scores, key_heads, preferred_element_type=jnp.float32)
        * scale_factor
    )
    key_dense = (
        jnp.einsum(
            "ghqk,gqhd->khd", dense_scores, dense_queries, preferred_element_type=jnp.float32
        )
        * scale_factor
    )
    value_dense = jnp.einsum(
        "ghqk,gqhd->khd",
        dense_soft.astype(jnp.bfloat16),
        dense_grads,
        preferred_element_type=jnp.float32,
    )
    query_grad = query_sparse + place_rows(place_map, query_dense)
    key_grad = key_blocks.transpose(0, 2, 1, 3).reshape(LEN, H * HD) + key_dense.reshape(
        LEN, H * HD
    )
    value_grad = value_blocks.transpose(0, 2, 1, 3).reshape(LEN, H * HD) + value_dense.reshape(
        LEN, H * HD
    )
    return (query_grad.reshape(block_count * BLK, H * HD), key_grad, value_grad)


def shards(
    inputs,
    cotangent,
    query_weight,
    query_bias,
    key_weight,
    value_weight,
    value_bias,
    output_weight,
    output_bias,
    first_gain,
    first_shift,
    inner_weight,
    inner_bias,
    outer_weight,
    outer_bias,
    second_gain,
    second_shift,
    lengths,
    random_blocks,
    threshold,
):
    params = (
        lax.all_gather(query_weight, ("dp", "ctx"), axis=0, tiled=True),
        lax.all_gather(query_bias, ("dp", "ctx"), axis=0, tiled=True),
        lax.all_gather(key_weight, ("dp", "ctx"), axis=0, tiled=True),
        lax.all_gather(value_weight, ("dp", "ctx"), axis=0, tiled=True),
        lax.all_gather(value_bias, ("dp", "ctx"), axis=0, tiled=True),
        lax.all_gather(output_weight, ("dp", "ctx"), axis=0, tiled=True),
        lax.all_gather(output_bias, ("dp", "ctx"), axis=0, tiled=True),
        lax.all_gather(first_gain, ("dp", "ctx"), axis=0, tiled=True),
        lax.all_gather(first_shift, ("dp", "ctx"), axis=0, tiled=True),
        lax.all_gather(inner_weight, ("dp", "ctx"), axis=0, tiled=True),
        lax.all_gather(inner_bias, ("dp", "ctx"), axis=0, tiled=True),
        lax.all_gather(outer_weight, ("dp", "ctx"), axis=0, tiled=True),
        lax.all_gather(outer_bias, ("dp", "ctx"), axis=0, tiled=True),
        lax.all_gather(second_gain, ("dp", "ctx"), axis=0, tiled=True),
        lax.all_gather(second_shift, ("dp", "ctx"), axis=0, tiled=True),
    )
    (
        full_query,
        full_qbias,
        full_key,
        full_value,
        full_vbias,
        full_out,
        full_obias,
        full_gain_one,
        full_shift_one,
        full_inner,
        full_ibias,
        full_outer,
        full_outer_bias,
        full_gain_two,
        full_shift_two,
    ) = params
    seq_here, local_len, model_width = inputs.shape
    local_blocks = local_len // BLK
    ctx_rank = lax.axis_index("ctx")
    first_block = ctx_rank * local_blocks
    random_local = lax.dynamic_slice_in_dim(random_blocks, first_block, local_blocks, 1)
    token_rows = inputs.reshape(seq_here * local_len, model_width)
    queries = (matmul(token_rows, full_query) + full_qbias).astype(jnp.bfloat16)
    keys_local = matmul(token_rows, full_key).astype(jnp.bfloat16)
    values_local = (matmul(token_rows, full_value) + full_vbias).astype(jnp.bfloat16)
    keys_whole, values_whole = (
        lax.all_gather(
            keys_local.reshape(seq_here, local_len, model_width), "ctx", axis=1, tiled=True
        ),
        lax.all_gather(
            values_local.reshape(seq_here, local_len, model_width), "ctx", axis=1, tiled=True
        ),
    )
    queries_seq = queries.reshape(seq_here, local_len, model_width)
    query_positions = ctx_rank * local_len + jnp.arange(local_len)

    def forward_seq(running_top, seq_item):
        query_block, key_block, value_block, length, random_here = seq_item
        mixture, log_total, top_here = attend_piece(
            query_block, key_block, value_block, length, random_here, first_block
        )
        return (jnp.maximum(running_top, top_here), (mixture, log_total))

    top_local, (attended, log_totals) = lax.scan(
        forward_seq,
        jnp.full((H,), neg_large, jnp.float32),
        (queries_seq, keys_whole, values_whole, lengths, random_local),
    )
    logit_maxima = lax.pmax(top_local, ("dp", "ctx"))
    attended_rows = attended.reshape(seq_here * local_len, model_width)
    first_sum = token_rows.astype(jnp.float32) + matmul(attended_rows, full_out) + full_obias
    normed = layer_norm(first_sum, full_gain_one, full_shift_one)
    normed_low = normed.astype(jnp.bfloat16)
    pre_act = matmul(normed_low, full_inner) + full_ibias
    activated = gelu_exact(pre_act).astype(jnp.bfloat16)
    second_sum = normed + matmul(activated, full_outer) + full_outer_bias
    result = layer_norm(second_sum, full_gain_two, full_shift_two)
    output = result.reshape(seq_here, local_len, model_width).astype(jnp.bfloat16)
    back_params = (
        lax.all_gather(query_weight, ("dp", "ctx"), axis=0, tiled=True),
        lax.all_gather(query_bias, ("dp", "ctx"), axis=0, tiled=True),
        lax.all_gather(key_weight, ("dp", "ctx"), axis=0, tiled=True),
        lax.all_gather(value_weight, ("dp", "ctx"), axis=0, tiled=True),
        lax.all_gather(value_bias, ("dp", "ctx"), axis=0, tiled=True),
        lax.all_gather(output_weight, ("dp", "ctx"), axis=0, tiled=True),
        lax.all_gather(output_bias, ("dp", "ctx"), axis=0, tiled=True),
        lax.all_gather(first_gain, ("dp", "ctx"), axis=0, tiled=True),
        lax.all_gather(first_shift, ("dp", "ctx"), axis=0, tiled=True),
        lax.all_gather(inner_weight, ("dp", "ctx"), axis=0, tiled=True),
        lax.all_gather(inner_bias, ("dp", "ctx"), axis=0, tiled=True),
        lax.all_gather(outer_weight, ("dp", "ctx"), axis=0, tiled=True),
        lax.all_gather(outer_bias, ("dp", "ctx"), axis=0, tiled=True),
        lax.all_gather(second_gain, ("dp", "ctx"), axis=0, tiled=True),
        lax.all_gather(second_shift, ("dp", "ctx"), axis=0, tiled=True),
    )
    back_query = back_params[0]
    back_key = back_params[2]
    back_value = back_params[3]
    back_out = back_params[5]
    back_gain_one = back_params[7].astype(jnp.float32)
    back_shift_one = back_params[8].astype(jnp.float32)
    back_inner = back_params[9]
    back_outer = back_params[11]
    back_gain_two = back_params[13].astype(jnp.float32)
    back_shift_two = back_params[14].astype(jnp.float32)
    valid_rows = (query_positions[None, :] < lengths[:, None]).astype(jnp.float32)
    cot_rows = (cotangent.astype(jnp.float32) * valid_rows[:, :, None]).reshape(
        seq_here * local_len, model_width
    )
    second_pull = jax.vjp(layer_norm, second_sum, back_gain_two, back_shift_two)[1]
    grad_second, second_gain_grad, second_shift_grad = second_pull(cot_rows)
    grad_outer_low = grad_second.astype(jnp.bfloat16)
    outer_bias_grad = column_sums(grad_outer_low)
    outer_weight_grad = contract_rows(activated, grad_outer_low)
    grad_activated = times_transposed(grad_outer_low, back_outer)
    grad_pre = jax.vjp(gelu_exact, pre_act)[1](grad_activated)[0]
    grad_pre_low = grad_pre.astype(jnp.bfloat16)
    inner_bias_grad = column_sums(grad_pre_low)
    inner_weight_grad = contract_rows(normed_low, grad_pre_low)
    grad_normed = grad_second + times_transposed(grad_pre_low, back_inner)
    first_pull = jax.vjp(layer_norm, first_sum, back_gain_one, back_shift_one)[1]
    grad_first, first_gain_grad, first_shift_grad = first_pull(grad_normed)
    grad_proj_low = grad_first.astype(jnp.bfloat16)
    output_bias_grad = column_sums(grad_proj_low)
    output_weight_grad = contract_rows(attended_rows, grad_proj_low)
    grad_attended = (
        times_transposed(grad_proj_low, back_out)
        .astype(jnp.bfloat16)
        .reshape(seq_here, local_len, model_width)
    )

    def backward_seq(unused_state, seq_item):
        query_block, key_block, value_block, length, random_here, log_total, grad_block = seq_item
        query_part, key_part, value_part = attend_back(
            query_block,
            grad_block,
            log_total,
            key_block,
            value_block,
            length,
            random_here,
            first_block,
        )
        return (unused_state, (query_part, key_part, value_part))

    unused_final, (query_parts, key_parts, value_parts) = lax.scan(
        backward_seq,
        jnp.zeros((), jnp.float32),
        (queries_seq, keys_whole, values_whole, lengths, random_local, log_totals, grad_attended),
    )
    key_sums, value_sums = (
        lax.psum_scatter(
            key_parts.astype(jnp.bfloat16), "ctx", scatter_dimension=1, tiled=True
        ).astype(jnp.float32),
        lax.psum_scatter(
            value_parts.astype(jnp.bfloat16), "ctx", scatter_dimension=1, tiled=True
        ).astype(jnp.float32),
    )
    grad_queries = query_parts.reshape(seq_here * local_len, model_width).astype(jnp.bfloat16)
    grad_keys = key_sums.reshape(seq_here * local_len, model_width).astype(jnp.bfloat16)
    grad_values = value_sums.reshape(seq_here * local_len, model_width).astype(jnp.bfloat16)
    query_weight_grad = contract_rows(token_rows, grad_queries)
    query_bias_grad = column_sums(grad_queries)
    key_weight_grad = contract_rows(token_rows, grad_keys)
    value_weight_grad = contract_rows(token_rows, grad_values)
    value_bias_grad = column_sums(grad_values)
    input_rows = (
        grad_first
        + times_transposed(grad_queries, back_query)
        + times_transposed(grad_keys, back_key)
        + times_transposed(grad_values, back_value)
    )
    input_grad = input_rows.reshape(seq_here, local_len, model_width)
    (
        query_weight_grad,
        query_bias_grad,
        key_weight_grad,
        value_weight_grad,
        value_bias_grad,
        output_weight_grad,
        output_bias_grad,
        first_gain_grad,
        first_shift_grad,
        inner_weight_grad,
        inner_bias_grad,
        outer_weight_grad,
        outer_bias_grad,
        second_gain_grad,
        second_shift_grad,
    ) = (
        lax.psum_scatter(query_weight_grad, ("dp", "ctx"), scatter_dimension=0, tiled=True),
        lax.psum_scatter(query_bias_grad, ("dp", "ctx"), scatter_dimension=0, tiled=True),
        lax.psum_scatter(key_weight_grad, ("dp", "ctx"), scatter_dimension=0, tiled=True),
        lax.psum_scatter(value_weight_grad, ("dp", "ctx"), scatter_dimension=0, tiled=True),
        lax.psum_scatter(value_bias_grad, ("dp", "ctx"), scatter_dimension=0, tiled=True),
        lax.psum_scatter(output_weight_grad, ("dp", "ctx"), scatter_dimension=0, tiled=True),
        lax.psum_scatter(output_bias_grad, ("dp", "ctx"), scatter_dimension=0, tiled=True),
        lax.psum_scatter(first_gain_grad, ("dp", "ctx"), scatter_dimension=0, tiled=True),
        lax.psum_scatter(first_shift_grad, ("dp", "ctx"), scatter_dimension=0, tiled=True),
        lax.psum_scatter(inner_weight_grad, ("dp", "ctx"), scatter_dimension=0, tiled=True),
        lax.psum_scatter(inner_bias_grad, ("dp", "ctx"), scatter_dimension=0, tiled=True),
        lax.psum_scatter(outer_weight_grad, ("dp", "ctx"), scatter_dimension=0, tiled=True),
        lax.psum_scatter(outer_bias_grad, ("dp", "ctx"), scatter_dimension=0, tiled=True),
        lax.psum_scatter(second_gain_grad, ("dp", "ctx"), scatter_dimension=0, tiled=True),
        lax.psum_scatter(second_shift_grad, ("dp", "ctx"), scatter_dimension=0, tiled=True),
    )
    clip_limit = threshold.astype(jnp.float32)[0] * 0.01
    factors = jnp.sqrt(clip_limit / jnp.maximum(logit_maxima, clip_limit))
    column_scale = jnp.repeat(factors, HD)
    query_weight_clipped = (query_weight.astype(jnp.float32) * column_scale[None, :]).astype(
        jnp.bfloat16
    )
    key_weight_clipped = (key_weight.astype(jnp.float32) * column_scale[None, :]).astype(
        jnp.bfloat16
    )
    bias_count = query_bias.shape[0]
    device_rank = lax.axis_index(("dp", "ctx"))
    bias_heads = (device_rank * bias_count + jnp.arange(bias_count)) // HD
    bias_scale = jnp.sum(
        jnp.where(bias_heads[:, None] == jnp.arange(H)[None, :], factors[None, :], 0.0), axis=1
    )
    query_bias_clipped = (query_bias.astype(jnp.float32) * bias_scale).astype(jnp.bfloat16)
    return (
        output,
        input_grad,
        query_weight_grad,
        query_bias_grad,
        key_weight_grad,
        value_weight_grad,
        value_bias_grad,
        output_weight_grad,
        output_bias_grad,
        first_gain_grad,
        first_shift_grad,
        inner_weight_grad,
        inner_bias_grad,
        outer_weight_grad,
        outer_bias_grad,
        second_gain_grad,
        second_shift_grad,
        query_weight_clipped,
        query_bias_clipped,
        key_weight_clipped,
        logit_maxima,
    )


def solution(mesh):
    in_specs = (
        P("dp", "ctx", None),
        P("dp", "ctx", None),
        P(("dp", "ctx"), None),
        P(("dp", "ctx")),
        P(("dp", "ctx"), None),
        P(("dp", "ctx"), None),
        P(("dp", "ctx")),
        P(("dp", "ctx"), None),
        P(("dp", "ctx")),
        P(("dp", "ctx")),
        P(("dp", "ctx")),
        P(("dp", "ctx"), None),
        P(("dp", "ctx")),
        P(("dp", "ctx"), None),
        P(("dp", "ctx")),
        P(("dp", "ctx")),
        P(("dp", "ctx")),
        P("dp"),
        P("dp", None, None, None),
        P(),
    )
    out_specs = (
        P("dp", "ctx", None),
        P("dp", "ctx", None),
        P(("dp", "ctx"), None),
        P(("dp", "ctx")),
        P(("dp", "ctx"), None),
        P(("dp", "ctx"), None),
        P(("dp", "ctx")),
        P(("dp", "ctx"), None),
        P(("dp", "ctx")),
        P(("dp", "ctx")),
        P(("dp", "ctx")),
        P(("dp", "ctx"), None),
        P(("dp", "ctx")),
        P(("dp", "ctx"), None),
        P(("dp", "ctx")),
        P(("dp", "ctx")),
        P(("dp", "ctx")),
        P(("dp", "ctx"), None),
        P(("dp", "ctx")),
        P(("dp", "ctx"), None),
        P(),
    )
    return jax.shard_map(shards, mesh=mesh, in_specs=in_specs, out_specs=out_specs, check_vma=False)
```

profile of v0, /device:TPU:0, one launch (start us, length us, event | category | flops | bytes accessed | tf_op | source)
XLA Modules:
  0.0 1553.7 jit_solution(18072110034240122984)
XLA Ops:
  9.5 58.4 %all-gather.13.cloned.1.call-done = bf16[768,768]{1,0:T(8,128)(2,1)} async-done(((bf16[24,768]{1,0:T(8,128)(2,1)}), bf16[768,768]{1,0:T(8,128)(2,1)}) %all-gather.13.cloned.1.call-update) | async-done | bytes 1179664 | tf_op jit(solution)/shard_map/all_gather | solution.py:290
  78.7 39.7 %all-reduce.19 = (bf16[768]{0:T(1024)(128)(2,1)S(1)}, bf16[768]{0:T(1024)(128)(2,1)S(1)}, bf16[768]{0:T(1024)(128)(2,1)S(1)}, bf16[768]{0:T(1024)(128)(2,1)S(1)}...) all-reduce(bf16[768]{0:T(1024)(128)(2,1)S(1)} %dynamic-update-slice, ...), channel_id=1, replica_groups=mesh['dp'=16,'ctx'=2] {'dp','ctx'}, use_global_device_ids=true, to_apply=%add | all-reduce | flops 9216 | bytes 36864
  118.4 5.7 all-gather.11.cloned.1.call-done
  135.2 45.0 %all-gather.15.cloned.1.call-done = bf16[768,768]{1,0:T(8,128)(2,1)} async-done(((bf16[24,768]{1,0:T(8,128)(2,1)}), bf16[768,768]{1,0:T(8,128)(2,1)}) %all-gather.15.cloned.1.call-update) | async-done | bytes 1179664 | tf_op jit(solution)/shard_map/all_gather | solution.py:288
  188.2 20.1 %all-gather.25.cloned.1.call-done = bf16[1024,768]{1,0:T(8,128)(2,1)} async-done(((bf16[512,768]{1,0:T(8,128)(2,1)}), bf16[1024,768]{1,0:T(8,128)(2,1)}) %all-gather.25.cloned.1.call-update) | async-done | bytes 1572880 | tf_op jit(solution)/shard_map/all_gather | solution.py:331
  208.4 5.9 reshape.741
  228.2 9.4 all-gather.23.cloned.1.call-done
  240.2 5.9 fusion.33
  248.4 3.6 select_reduce_fusion.2
  254.6 5.9 reshape.740
  260.5 4.6 copy.271
  265.1 9.7 gather_fusion.2
  274.8 10.7 gather_fusion.1
  285.5 13.2 fusion.6
  298.8 17.0 %select_reduce_fusion = (f32[12]{0:T(128)}, f32[8,12,64]{2,1,0:T(8,128)S(1)}) fusion(f32[8,12,64,8,64]{2,4,3,1,0:T(8,128)S(1)} %get-tuple-element.243, pred[8,64]{1,0:T(8,128)(4,1)S(1)} %add_compare_fusion.1, pred[8,12,8,64]{3,2,1,0:T(8,128)(4,1)S(1)} %fusion.48, f32[8,12,64]{2,1,0:T(8,128)S(1)} %get-tuple-element.242), kind=kLoop, calls=%fused_computation.8 | loop fusion | flops 22013940 | bytes 12681776 | tf_op jit(solution)/shard_map/while/body/eval_jaxpr/reduce_max | solution.py:123
  315.8 13.5 fusion.18
  335.0 25.2 %all-gather.19.cloned.1.call-done = bf16[768,3072]{1,0:T(8,128)(2,1)} async-done(((bf16[24,3072]{1,0:T(8,128)(2,1)}), bf16[768,3072]{1,0:T(8,128)(2,1)}) %all-gather.19.cloned.1.call-update) | async-done | bytes 4718608 | tf_op jit(solution)/shard_map/all_gather | solution.py:297
  360.2 19.8 %multiply_convert_fusion.2 = (bf16[512,3072]{1,0:T(8,128)(2,1)}, f32[512,3072]{1,0:T(8,128)}, f32[512,3072]{1,0:T(8,128)}) fusion(f32[3072]{0:T(1024)S(1)} %convert_element_type.202, bf16[768,3072]{1,0:T(8,128)(2,1)} %all-gather.19.cloned.1.call-done, f32[512,768]{1,0:T(8,128)S(1)} %get-tuple-element.245, f32[768]{0:T(1024)S(1)} %convert_element_type.200, ...), kind=kOutput, calls=%fused_computation.33 | convolution fusion | flops 2521694208 | bytes 22042624 | tf_op jit(solution)/shard_map/dot_general | solution.py:28
  380.0 45.5 %all-gather.21.cloned.1.call-done = bf16[3072,768]{1,0:T(8,128)(2,1)} async-done(((bf16[96,768]{1,0:T(8,128)(2,1)}), bf16[3072,768]{1,0:T(8,128)(2,1)}) %all-gather.21.cloned.1.call-update) | async-done | bytes 4718608 | tf_op jit(solution)/shard_map/all_gather | solution.py:299
  425.6 6.1 fusion.78
  435.9 8.9 convert_reduce_fusion
  444.8 3.7 multiply_reduce_fusion.2
  455.9 17.9 %fusion.2 = f32[8,12,8,64,64]{4,3,2,1,0:T(8,128)} fusion(f32[8,12,64]{2,1,0:T(8,128)S(1)} %copy_select_fusion.3, f32[8,12,64,8,64]{2,4,3,1,0:T(8,128)} %copy-done.2, pred[8,12,8,64]{3,2,1,0:T(8,128)(4,1)S(1)} %fusion.48, bf16[8,64,12,64]{1,0,3,2:T(8,128)(2,1)S(1)} %reshape.637, pred[8]{0:T(512)(128)(4,1)S(1)} %get-tuple-element.231), kind=kOutput, calls=%fused_computation.17 | convolution fusion | flops 415629312 | bytes 26025992 | tf_op jit(solution)/shard_map/while/body/eval_jaxpr/ihqck,iqhd->ihckd/dot_general | solution.py:210
  473.8 22.1 %multiply_reduce_fusion = (f32[8,12,64]{2,1,0:T(8,128)S(1)}, f32[8,12,64,8,64]{2,4,3,1,0:T(8,128)}) fusion(f32[8,12,64]{2,1,0:T(8,128)S(1)} %copy_select_fusion.3, f32[8,12,64,8,64]{2,4,3,1,0:T(8,128)} %copy-done.2, pred[8,12,8,64]{3,2,1,0:T(8,128)(4,1)S(1)} %fusion.48, bf16[8,12,8,64,64]{4,3,2,1,0:T(8,128)(2,1)} %bitcast.257, ...), kind=kOutput, calls=%fused_computation.10 | convolution fusion | flops 418768896 | bytes 32342024 | tf_op jit(solution)/shard_map/while/body/eval_jaxpr/iqhd,ihckd->ihqck/dot_general | solution.py:195
  510.3 121.7 %scatter_fusion.1 = f32[16,12,64,64]{3,2,1,0:T(8,128)} fusion(f32[16,12,64,64]{3,2,1,0:T(8,128)} %broadcast.626.clone.1, s32[768]{0:T(1024)S(1)} %copy-done.5, f32[768,64,64]{2,1,0:T(8,128)} %bitcast.253), kind=kCustom, calls=%fused_computation.7 | custom fusion | flops 3145728 | bytes 37754880 | tf_op jit(solution)/shard_map/while/body/eval_jaxpr/scatter-add | solution.py:219
  632.0 6.9 copy.208
  639.0 6.3 reshape.640
  645.3 3.6 fusion.16
  649.0 17.1 %multiply_convert_fusion = bf16[8,12,64,8,64]{2,4,3,1,0:T(8,128)(2,1)S(1)} fusion(f32[8,12,64,8,64]{2,4,3,1,0:T(8,128)} %get-tuple-element.251, f32[8,12,64]{2,1,0:T(8,128)S(1)} %get-tuple-element.250, f32[8,12,64]{2,1,0:T(8,128)S(1)} %copy_select_fusion.3, f32[8,12,64,8,64]{2,4,3,1,0:T(8,128)} %copy-done.2, pred[8,12,8,64]{3,2,1,0:T(8,128)(4,1)S(1)} %fusion.48), kind=kLoop, calls=%fused_computation.9 | loop fusion | flops 18874368 | bytes 31555584 | tf_op jit(solution)/shard_map/while/body/eval_jaxpr/convert_element_type | solution.py:199
  666.1 10.5 broadcast_multiply_fusion
  678.2 3.4 broadcast.626.clone
  681.7 121.9 %scatter_fusion = f32[16,12,64,64]{3,2,1,0:T(8,128)} fusion(f32[16,12,64,64]{3,2,1,0:T(8,128)} %broadcast.626.clone, s32[768]{0:T(1024)S(1)} %copy-done.5, f32[768,64,64]{2,1,0:T(8,128)} %bitcast.250), kind=kCustom, calls=%fused_computation.6 | custom fusion | flops 3145728 | bytes 37754880 | tf_op jit(solution)/shard_map/while/body/eval_jaxpr/scatter-add | solution.py:217
  803.6 7.0 copy.204
  810.5 6.5 reshape.638
  821.0 4.0 fusion.34
  829.8 12.6 convert_reduce_fusion.1
  850.2 3.6 fusion.80
  862.0 8.9 fusion.69
  872.1 8.2 fusion.81
  881.7 39.9 %pmax.7 = f32[12]{0:T(128)S(1)} all-reduce(f32[12]{0:T(128)S(1)} %maximum_maximum_fusion), channel_id=1, replica_groups=mesh['dp'=16,'ctx'=2] {'dp','ctx'}, use_global_device_ids=true, to_apply=%region_49.50 | all-reduce | flops 12 | bytes 96 | tf_op jit(solution)/shard_map/pmax | solution.py:353
  923.1 3.5 fusion.79
  926.8 41.1 %all-reduce.18 = (f32[768]{0:T(1024)S(1)}, f32[768]{0:T(1024)S(1)}, f32[768]{0:T(1024)S(1)}, f32[768]{0:T(1024)S(1)}, f32[768]{0:T(1024)S(1)}, /*index=5*/f32[30...) all-reduce(f32[768]{0:T(1024)S(1)} %reduce_sum.298, ...), channel_id=7, replica_groups=mesh['dp'=16,'ctx'=2] {'dp','ctx'}, use_global_device_ids=true, to_apply=%region_25.26.clone | all-reduce | flops 9216 | bytes 73728
  975.4 3.6 add_bitcast_fusion
  978.9 76.9 %reduce-scatter.19.cloned.1.call-done = f32[24,768]{1,0:T(8,128)} async-done(((f32[768,768]{1,0:T(8,128)}), f32[24,768]{1,0:T(8,128)}) %reduce-scatter.19.cloned.1.call-update) | async-done | bytes 73744 | tf_op jit(solution)/shard_map/reduce_scatter | solution.py:480
  1055.8 103.9 %reduce-scatter.29.cloned.1.call-done = f32[24,768]{1,0:T(8,128)} async-done(((f32[768,768]{1,0:T(8,128)}), f32[24,768]{1,0:T(8,128)}) %reduce-scatter.29.cloned.1.call-update) | async-done | bytes 73744
  1159.7 104.6 %reduce-scatter.27.cloned.1.call-done = f32[24,768]{1,0:T(8,128)} async-done(((f32[768,768]{1,0:T(8,128)}), f32[24,768]{1,0:T(8,128)}) %reduce-scatter.27.cloned.1.call-update) | async-done | bytes 73744
  1264.4 140.9 %reduce-scatter.21.cloned.1.call-done = f32[24,3072]{1,0:T(8,128)} async-done(((f32[768,3072]{1,0:T(8,128)}), f32[24,3072]{1,0:T(8,128)}) %reduce-scatter.21.cloned.1.call-update) | async-done | bytes 294928 | tf_op jit(solution)/shard_map/reduce_scatter | solution.py:484
  1405.3 141.6 %reduce-scatter.23.cloned.1.call-done = f32[96,768]{1,0:T(8,128)} async-done(((f32[3072,768]{1,0:T(8,128)}), f32[96,768]{1,0:T(8,128)}) %reduce-scatter.23.cloned.1.call-update) | async-done | bytes 294928 | tf_op jit(solution)/shard_map/reduce_scatter | solution.py:486
  (322 shorter events, 121.0 us)
Async XLA Ops:
  7.2 122.7 %copy-start = (s32[1,16,12,3]{1,0,3,2:T(1,128)S(1)}, s32[1,16,12,3]{1,0,3,2:T(1,128)}, u32[]{:S(2)}) copy-start(s32[1,16,12,3]{1,0,3,2:T(1,128)} %param.38) | copy-start | bytes 6916
  7.2 116.9 %copy-start.16 = (bf16[1,512,768]{2,1,0:T(8,128)(2,1)S(1)}, bf16[1,512,768]{2,1,0:T(8,128)(2,1)}, u32[]{:S(2)}) copy-start(bf16[1,512,768]{2,1,0:T(8,128)(2,1)} %param.20) | copy-start | bytes 2359300
  7.2 60.6 %all-gather.13.cloned.1.call-start = ((), (), s32[]{:S(2)}) async-start(), calls=%async_computation.9 | async-start | bytes 1216512 | tf_op jit(solution)/shard_map/all_gather | solution.py:290
  8.0 116.1 %all-gather.11.cloned.1.call-start = ((), (), s32[]{:S(2)}) async-start(), calls=%async_computation.8 | async-start | bytes 1216512 | tf_op jit(solution)/shard_map/all_gather | solution.py:291
  8.7 171.5 %all-gather.15.cloned.1.call-start = ((), (), s32[]{:S(2)}) async-start(), calls=%async_computation.10 | async-start | bytes 1216512 | tf_op jit(solution)/shard_map/all_gather | solution.py:288
  9.4 199.0 %all-gather.25.cloned.1.call-start = ((), (), s32[]{:S(2)}) async-start(), calls=%async_computation.20 | async-start | bytes 2359296 | tf_op jit(solution)/shard_map/all_gather | solution.py:331
  71.0 166.6 %all-gather.23.cloned.1.call-start = ((), (), s32[]{:S(2)}) async-start(), calls=%async_computation.19 | async-start | bytes 2359296 | tf_op jit(solution)/shard_map/all_gather | solution.py:334
  127.0 205.4 %all-gather.17.cloned.1.call-start = ((), (), s32[]{:S(2)}) async-start(), calls=%async_computation.11 | async-start | bytes 1216512 | tf_op jit(solution)/shard_map/all_gather | solution.py:293
  127.6 232.5 %all-gather.19.cloned.1.call-start = ((), (), s32[]{:S(2)}) async-start(), calls=%async_computation.12 | async-start | bytes 4866048 | tf_op jit(solution)/shard_map/all_gather | solution.py:297
  128.4 297.2 %all-gather.21.cloned.1.call-start = ((), (), s32[]{:S(2)}) async-start(), calls=%async_computation.13 | async-start | bytes 4866048 | tf_op jit(solution)/shard_map/all_gather | solution.py:299
  129.1 724.7 %reduce-scatter.17.cloned.1.call-start = ((), (), s32[]{:S(2)}) async-start(), calls=%async_computation.15 | async-start | bytes 2359296 | tf_op jit(solution)/shard_map/reduce_scatter | solution.py:439
  131.3 108.9 %copy-start.34 = (pred[1024]{0:T(1024)(128)(4,1)}, pred[1024]{0:T(1024)(128)(4,1)S(1)}, u32[]{:S(2)}) copy-start(pred[1024]{0:T(1024)(128)(4,1)S(1)} %iota_compare_fusion.3) | copy-start | bytes 3076
  132.3 116.1 %copy-start.49 = (pred[8,2]{1,0:T(8,128)(4,1)}, pred[8,2]{1,0:T(8,128)(4,1)S(1)}, u32[]{:S(2)}) copy-start(pred[8,2]{1,0:T(8,128)(4,1)S(1)} %copy.171) | copy-start | bytes 52
  132.3 316.2 %copy-start.43 = (f32[768]{0:T(1024)}, f32[768]{0:T(1024)S(1)}, u32[]{:S(2)}) copy-start(f32[768]{0:T(1024)S(1)} %convert_element_type.199) | copy-start | bytes 9220
  132.3 293.2 %copy-start.51 = (f32[768]{0:T(1024)}, f32[768]{0:T(1024)S(1)}, u32[]{:S(2)}) copy-start(f32[768]{0:T(1024)S(1)} %convert_element_type.200) | copy-start | bytes 9220
  187.4 21.0 %copy-start.21 = (bf16[2,64,12,64]{3,1,2,0:T(8,128)(2,1)}, bf16[2,64,12,64]{3,1,2,0:T(8,128)(2,1)S(1)}, u32[]{:S(2)}) copy-start(bf16[2,64,12,64]{3,1,2,0:T(8,128)(2,1)S(1)} %gather_fusion) | copy-start | bytes 589828
  285.5 30.3 %slice-start = ((s8[12582912]{0:T(1024)(128)(4,1)}), s8[4194304]{0:T(1024)(128)(4,1)S(1)}, s32[]{:S(2)}) async-start(s8[12582912]{0:T(1024)(128)(4,1)} %bitcast.258), calls=%async_computation.24 | async-start | bytes 8388608
  285.5 30.3 %slice-start.1 = ((s8[12582912]{0:T(1024)(128)(4,1)}), s8[4194304]{0:T(1024)(128)(4,1)S(1)}, s32[]{:S(2)}) async-start(s8[12582912]{0:T(1024)(128)(4,1)} %bitcast.258), calls=%async_computation.25 | async-start | bytes 8388608
  298.7 17.1 %copy-start.2 = (f32[8,12,64,8,64]{2,4,3,1,0:T(8,128)}, f32[8,12,64,8,64]{2,4,3,1,0:T(8,128)S(1)}, u32[]{:S(2)}) copy-start(f32[8,12,64,8,64]{2,4,3,1,0:T(8,128)S(1)} %get-tuple-element.243) | copy-start | bytes 37748740
  331.6 48.4 %copy-start.22 = (bf16[512,768]{0,1:T(8,128)(2,1)}, bf16[512,768]{0,1:T(8,128)(2,1)S(1)}, u32[]{:S(2)}) copy-start(bf16[512,768]{0,1:T(8,128)(2,1)S(1)} %convert_element_type.197) | copy-start | bytes 2359300
  334.6 113.9 %copy-start.19 = (f32[512,768]{1,0:T(8,128)}, f32[512,768]{1,0:T(8,128)S(1)}, u32[]{:S(2)}) copy-start(f32[512,768]{1,0:T(8,128)S(1)} %get-tuple-element.245) | copy-start | bytes 4718596
  334.6 113.9 %copy-start.36 = (f32[512]{0:T(512)}, f32[512]{0:T(512)S(1)}, u32[]{:S(2)}) copy-start(f32[512]{0:T(512)S(1)} %broadcast_multiply_fusion.2) | copy-start | bytes 6148
  335.0 113.6 %copy-start.47 = (f32[512]{0:T(512)}, f32[512]{0:T(512)S(1)}, u32[]{:S(2)}) copy-start(f32[512]{0:T(512)S(1)} %fusion.58) | copy-start | bytes 6148
  473.8 24.1 %copy-start.56 = (pred[2]{0:T(512)(128)(4,1)S(1)}, pred[2]{0:T(512)(128)(4,1)}, u32[]{:S(2)}) copy-start(pred[2]{0:T(512)(128)(4,1)} %copy-done.55) | copy-start | bytes 10
  473.8 24.3 %copy-start.20 = (bf16[1024,768]{0,1:T(8,128)(2,1)S(1)}, bf16[1024,768]{0,1:T(8,128)(2,1)}, u32[]{:S(2)}) copy-start(bf16[1024,768]{0,1:T(8,128)(2,1)} %copy.172) | copy-start | bytes 4718596
  648.9 209.0 %reduce-scatter.15.cloned.1.call-start = ((), (), s32[]{:S(2)}) async-start(), calls=%async_computation.14 | async-start | bytes 2359296 | tf_op jit(solution)/shard_map/reduce_scatter | solution.py:436
  649.0 17.1 %copy-start.9 = (bf16[8,64,12,64,1]{3,1,4,2,0:T(8,128)(2,1)S(1)}, bf16[8,64,12,64,1]{3,1,4,2,0:T(8,128)(2,1)}, u32[]{:S(2)}) copy-start(bf16[8,64,12,64,1]{3,1,4,2,0:T(8,128)(2,1)} %copy.215) | copy-start | bytes 2359300
  821.0 158.0 %reduce-scatter.25.cloned.1.call-start = ((), (), s32[]{:S(2)}) async-start(), calls=%async_computation.21 | async-start | bytes 2433024
  850.1 205.7 %reduce-scatter.19.cloned.1.call-start = ((), (), s32[]{:S(2)}) async-start(), calls=%async_computation.16 | async-start | bytes 2433024 | tf_op jit(solution)/shard_map/reduce_scatter | solution.py:480
  853.8 305.9 %reduce-scatter.29.cloned.1.call-start = ((), (), s32[]{:S(2)}) async-start(), calls=%async_computation.23 | async-start | bytes 2433024
  857.8 406.5 %reduce-scatter.27.cloned.1.call-start = ((), (), s32[]{:S(2)}) async-start(), calls=%async_computation.22 | async-start | bytes 2433024
  861.9 543.4 %reduce-scatter.21.cloned.1.call-start = ((), (), s32[]{:S(2)}) async-start(), calls=%async_computation.17 | async-start | bytes 9732096 | tf_op jit(solution)/shard_map/reduce_scatter | solution.py:484
  870.9 676.0 %reduce-scatter.23.cloned.1.call-start = ((), (), s32[]{:S(2)}) async-start(), calls=%async_computation.18 | async-start | bytes 9732096 | tf_op jit(solution)/shard_map/reduce_scatter | solution.py:486
  880.3 41.5 %copy-start.61 = (bf16[24]{0:T(256)(128)(2,1)S(1)}, bf16[24]{0:T(256)(128)(2,1)}, u32[]{:S(2)}) copy-start(bf16[24]{0:T(256)(128)(2,1)} %param.23) | copy-start | bytes 148
  880.3 42.0 %copy-start.29 = (bf16[24,768]{1,0:T(8,128)(2,1)S(1)}, bf16[24,768]{1,0:T(8,128)(2,1)}, u32[]{:S(2)}) copy-start(bf16[24,768]{1,0:T(8,128)(2,1)} %param.24) | copy-start | bytes 110596
  880.3 42.0 %copy-start.30 = (bf16[24,768]{1,0:T(8,128)(2,1)S(1)}, bf16[24,768]{1,0:T(8,128)(2,1)}, u32[]{:S(2)}) copy-start(bf16[24,768]{1,0:T(8,128)(2,1)} %param.22) | copy-start | bytes 110596
  880.4 46.2 %copy-start.13 = (bf16[1,512,768]{1,2,0:T(8,128)(2,1)S(1)}, bf16[1,512,768]{1,2,0:T(8,128)(2,1)}, u32[]{:S(2)}) copy-start(bf16[1,512,768]{1,2,0:T(8,128)(2,1)} %reduce-scatter.17.cloned.1.call-done) | copy-start | bytes 2359300
  880.4 46.4 %copy-start.40 = (f32[768]{0:T(1024)S(1)}, f32[768]{0:T(1024)}, u32[]{:S(2)}) copy-start(f32[768]{0:T(1024)} %get-tuple-element.198) | copy-start | bytes 9220
  880.4 46.4 %copy-start.41 = (f32[768]{0:T(1024)S(1)}, f32[768]{0:T(1024)}, u32[]{:S(2)}) copy-start(f32[768]{0:T(1024)} %get-tuple-element.219) | copy-start | bytes 9220
  880.4 46.4 %copy-start.42 = (f32[768]{0:T(1024)S(1)}, f32[768]{0:T(1024)}, u32[]{:S(2)}) copy-start(f32[768]{0:T(1024)} %get-tuple-element.223) | copy-start | bytes 9220
  880.4 46.4 %copy-start.46 = (f32[3072]{0:T(1024)S(1)}, f32[3072]{0:T(1024)}, u32[]{:S(2)}) copy-start(f32[3072]{0:T(1024)} %get-tuple-element.221) | copy-start | bytes 36868
  880.4 46.4 %copy-start.53 = (f32[768]{0:T(1024)S(1)}, f32[768]{0:T(1024)}, u32[]{:S(2)}) copy-start(f32[768]{0:T(1024)} %get-tuple-element.196) | copy-start | bytes 9220
  880.4 46.4 %copy-start.54 = (f32[768]{0:T(1024)S(1)}, f32[768]{0:T(1024)}, u32[]{:S(2)}) copy-start(f32[768]{0:T(1024)} %get-tuple-element.200) | copy-start | bytes 9220
  880.4 94.9 %copy-start.11 = (f32[512,768]{1,0:T(8,128)S(1)}, f32[512,768]{1,0:T(8,128)}, u32[]{:S(2)}) copy-start(f32[512,768]{1,0:T(8,128)} %copy-done.10) | copy-start | bytes 4718596
  880.4 94.9 %copy-start.39 = (f32[512]{0:T(512)S(1)}, f32[512]{0:T(512)}, u32[]{:S(2)}) copy-start(f32[512]{0:T(512)} %copy-done.38) | copy-start | bytes 6148
  881.7 91.5 %copy-start.28 = (bf16[1,512,768]{1,2,0:T(8,128)(2,1)S(1)}, bf16[1,512,768]{1,2,0:T(8,128)(2,1)}, u32[]{:S(2)}) copy-start(bf16[1,512,768]{1,2,0:T(8,128)(2,1)} %reduce-scatter.15.cloned.1.call-done) | copy-start | bytes 2359300
  921.6 57.3 %copy-start.62 = (f32[12]{0:T(128)}, f32[12]{0:T(128)S(1)}, u32[]{:S(2)}) copy-start(f32[12]{0:T(128)S(1)} %pmax.7) | copy-start | bytes 148
  973.2 573.7 %copy-start.1 = (s32[1,16,12,3]{1,0,3,2:T(1,128)S(1)}, s32[1,16,12,3]{1,0,3,2:T(1,128)}, u32[]{:S(2)}) copy-start(s32[1,16,12,3]{1,0,3,2:T(1,128)} %param.38) | copy-start | bytes 6916
  (37 other events, 194.0 us)
Sparse Core Ops, SparseCore 0:
  11.0 56.8 all-gather.12
  70.8 53.2 all-gather.10
  127.0 53.1 all-gather.14
  182.2 26.1 all-gather.24
  210.4 27.2 all-gather.22
  240.4 54.1 all-gather.16
  297.5 62.6 all-gather.18
  363.1 62.4 all-gather.20
  649.0 25.0 reduce-scatter.16
  821.1 25.0 reduce-scatter.14
  852.0 99.0 reduce-scatter.24
  957.7 98.1 reduce-scatter.18
  1061.7 98.0 reduce-scatter.28
  1166.3 98.0 reduce-scatter.26
  1270.7 134.5 reduce-scatter.20
  1412.6 134.2 reduce-scatter.22
where the time goes:
time: 1560 us; the launch traced here: 1550 us
  waiting for transfers between devices  781 us (50%)
  other arithmetic  309 us (20%)
  matrix products  191 us (12%)
  local copies, waits for them, and re-layouts  133 us (9%)
  blocking collectives  121 us (8%)
  between operations  16.9 us (1%)
    scatter-add x2, other arithmetic, attend_back(): jnp.zeros((NB, H, BLK, HD), jnp.float32).at[safe_ids, head_ids]  244 us
    unnamed x19, waiting for transfers between devices  213 us
    reduce_scatter x1, waiting for transfers between devices, shards(): lax.psum_scatter(outer_weight_grad, ('dp', 'ctx'), scatter_dimension=0, t...  142 us
    reduce_scatter x1, waiting for transfers between devices, shards(): lax.psum_scatter(inner_weight_grad, ('dp', 'ctx'), scatter_dimension=0, t...  141 us
    unnamed x2, blocking collectives  80.8 us
    reduce_scatter x1, waiting for transfers between devices, shards(): lax.psum_scatter(output_weight_grad, ('dp', 'ctx'), scatter_dimension=0,...  76.9 us
    all_gather x1, waiting for transfers between devices, shards(): lax.all_gather(key_weight, ('dp', 'ctx'), axis=0, tiled=True)  58.4 us
    all_gather x1, waiting for transfers between devices, shards(): lax.all_gather(outer_weight, ('dp', 'ctx'), axis=0, tiled=True)  45.5 us
  transfers between devices with their start and end apart: 16, of which 12 were waited for; matrix products, arithmetic and copies ran while one was open for 26% of the time, Pallas kernels for 0%

commit v1 on v0

v1 whole, which is shorter than its diff:
```python
import functools

import jax
import jax.numpy as jnp
import numpy as np
from jax import lax
from jax.experimental import pallas as pl
from jax.experimental.pallas import tpu as pltpu
from jax.sharding import PartitionSpec as P

H = 12
HD = 64
BLK = 64
LEN = 1024
NB = 16
D = 768
FF = 3072

norm_eps = 1e-12
neg_large = -1e30
bf16 = jnp.bfloat16
f32 = jnp.float32
ANY = pl.BlockSpec(memory_space=pl.ANY)
INVMEM = pl.BlockSpec(memory_space=pltpu.VMEM)
INSMEM = pl.BlockSpec(memory_space=pltpu.SMEM)
MESH = pl.DeviceIdType.MESH


def dot_nn(a, b):
    return jnp.dot(a, b, preferred_element_type=f32)


def dot_nt(a, b):
    return lax.dot_general(a, b, (((1,), (1,)), ((), ())), preferred_element_type=f32)


def dot_tn(a, b):
    return lax.dot_general(a, b, (((0,), (0,)), ((), ())), preferred_element_type=f32)


def ds128(index, width):
    return pl.ds(pl.multiple_of(index * width, width), width)


class Place:
    def __init__(self, nz):
        self.nz = nz
        dp = lax.axis_index("dp")
        self.y = lax.axis_index("ctx")
        self.c = lax.rem(dp, 2)
        self.x = lax.rem(lax.div(dp, 2), 2)
        self.z = lax.div(dp, 4)

    def at(self, z=None, x=None, c=None, y=None):
        z = self.z if z is None else z
        x = self.x if x is None else x
        c = self.c if c is None else c
        y = self.y if y is None else y
        return ((z * 2 + x) * 2 + c, y)

    def z_off(self, k):
        return lax.rem(self.z + k, self.nz)

    def peers(self):
        return (
            [self.at(z=self.z_off(k)) for k in range(1, self.nz)]
            + [self.at(x=1 - self.x), self.at(y=1 - self.y), self.at(c=1 - self.c)]
        )


def entry_barrier(place):
    barrier = pltpu.get_barrier_semaphore()
    peers = place.peers()
    for peer in peers:
        pl.semaphore_signal(barrier, inc=1, device_id=peer, device_id_type=MESH)
    pl.semaphore_wait(barrier, len(peers))


class Remote:
    def __init__(self, send_sems, recv_sems):
        self.send_sems, self.recv_sems, self.used, self.copies = send_sems, recv_sems, 0, []

    def make(self, src, dst, peer):
        k = self.used
        self.used += 1
        copy = pltpu.make_async_remote_copy(
            src_ref=src, dst_ref=dst, send_sem=self.send_sems.at[k], recv_sem=self.recv_sems.at[k],
            device_id=peer, device_id_type=MESH,
        )
        self.copies.append(copy)
        return copy

    def finish(self):
        for copy in self.copies:
            copy.wait_send()


class Gather:
    def __init__(self, remote, place, buf, width):
        z, x, c, y = place.z, place.x, place.c, place.y
        half = width // 2
        a, b = slice(0, half), slice(half, width)
        zs = range(1, place.nz)

        def make(ref, peer):
            return remote.make(ref, ref, peer)

        self.az = [make(buf.at[z, x, c, y, :, a], place.at(z=place.z_off(k))) for k in zs]
        self.ax = make(buf.at[:, x, c, y, :, a], place.at(x=1 - x))
        self.ay = make(buf.at[:, :, c, y, :, a], place.at(y=1 - y))
        self.by = make(buf.at[z, x, c, y, :, b], place.at(y=1 - y))
        self.bz = [make(buf.at[z, x, c, :, :, b], place.at(z=place.z_off(k))) for k in zs]
        self.bx = make(buf.at[:, x, c, :, :, b], place.at(x=1 - x))
        self.ca = make(buf.at[:, :, c, :, :, a], place.at(c=1 - c))
        self.cb = make(buf.at[:, :, c, :, :, b], place.at(c=1 - c))

    def step(self, n):
        if n == 0:
            self.by.start()
            for copy in self.az:
                copy.start()
        elif n == 1:
            self.by.wait_recv()
            for copy in self.bz:
                copy.start()
        elif n == 2:
            for copy in self.az:
                copy.wait_recv()
            self.ax.start()
        elif n == 3:
            for copy in self.bz:
                copy.wait_recv()
            self.bx.start()
        elif n == 4:
            self.ax.wait_recv()
            self.ay.start()
        elif n == 5:
            self.bx.wait_recv()
            self.cb.start()
        elif n == 6:
            self.ay.wait_recv()
            self.ca.start()
        elif n == 7:
            self.ca.wait_recv()
            self.cb.wait_recv()


def layer_norm_parts(rows):
    centre = rows - jnp.mean(rows, axis=-1, keepdims=True)
    spread = jnp.mean(centre * centre, axis=-1, keepdims=True)
    inverse = lax.rsqrt(spread + norm_eps)
    return centre * inverse, inverse


def head_lanes(rows, half):
    lane = lax.broadcasted_iota(jnp.int32, rows.shape, 1)
    return jnp.where((lane >= HD) == (half == 1), rows, jnp.zeros_like(rows))


def key_structure(seq_len, length):
    lane = lax.broadcasted_iota(jnp.int32, (seq_len, 128), 1)
    row = lax.broadcasted_iota(jnp.int32, (seq_len, 128), 0)
    own = lane == lax.shift_right_logical(row, 6)
    beyond = (lane == NB) & (row >= length)
    return jnp.where(own | beyond, 1.0, 0.0).astype(bf16)


def query_structure(compact):
    blocks = compact.shape[0]
    return jnp.broadcast_to(compact[:, None, :], (blocks, BLK, 128)).reshape(blocks * BLK, 128).astype(bf16)


def spread_vectors(tiles, width, pieces):
    rows = tiles.shape[1]
    total = pieces * width
    lane = lax.broadcasted_iota(jnp.int32, (128, total), 1).astype(f32)
    row = lax.broadcasted_iota(jnp.int32, (128, total), 0).astype(f32)
    owner = jnp.floor((lane + 0.5) * (1.0 / width))
    chooser = jnp.where(lane - owner * width == row, 1.0, 0.0).astype(bf16)
    wide = dot_nn(tiles.reshape(pieces * rows, 128), chooser).reshape(pieces, rows, total)
    lane3 = lax.broadcasted_iota(jnp.int32, (pieces, rows, total), 2).astype(f32)
    piece3 = lax.broadcasted_iota(jnp.int32, (pieces, rows, total), 0).astype(f32)
    mine = jnp.floor((lane3 + 0.5) * (1.0 / width)) == piece3
    return jnp.sum(jnp.where(mine, wide, 0.0), axis=0)


def forward_kernel(
    nz, local, length_ref, compact_ref, x_hbm, wq, wk, wv, wo, wi, wu, small,
    out_hbm, r1_hbm, u_hbm, r2_hbm, a_hbm, q_hbm, k_hbm, v_hbm, xf_hbm, lse_hbm, top_hbm, wa_hbm, wi_hbm, wu_hbm, vec_hbm,
    WA, WI, WU, SM, XF, Q, K, V, VT, AT, A, R1, R2, N1L, U, G, PB, S, E, VEC, IB, LSE, TOP, OUT,
    send_sems, recv_sems, local_sems, out_sems,
):
    place = Place(nz)
    z, x, c, y = place.z, place.x, place.c, place.y
    remote = Remote(send_sems, recv_sems)
    mine = (z, x, c, y)
    locals_ = [
        pltpu.make_async_copy(x_hbm, XF.at[y], local_sems.at[0]),
        pltpu.make_async_copy(wq, WA.at[(*mine, slice(None), slice(0, D))], local_sems.at[1]),
        pltpu.make_async_copy(wk, WA.at[(*mine, slice(None), slice(D, 2 * D))], local_sems.at[2]),
        pltpu.make_async_copy(wv, WA.at[(*mine, slice(None), slice(2 * D, 3 * D))], local_sems.at[3]),
        pltpu.make_async_copy(wo, WA.at[(*mine, slice(None), slice(3 * D, 4 * D))], local_sems.at[4]),
        pltpu.make_async_copy(wi, WI.at[mine], local_sems.at[5]),
        pltpu.make_async_copy(wu, WU.at[mine], local_sems.at[6]),
        pltpu.make_async_copy(small, SM.at[mine], local_sems.at[7]),
    ]
    for copy in locals_:
        copy.start()
    entry_barrier(place)
    for copy in locals_:
        copy.wait()

    outs = []

    def put(src, dst):
        copy = pltpu.make_async_copy(src, dst, out_sems.at[len(outs)])
        copy.start()
        outs.append(copy)

    xs = remote.make(XF.at[y], XF.at[y], place.at(y=1 - y))
    ga = Gather(remote, place, WA, 4 * D)
    gi = Gather(remote, place, WI, FF)
    gu = Gather(remote, place, WU, D)
    sz = [remote.make(SM.at[mine], SM.at[mine], place.at(z=place.z_off(k))) for k in range(1, nz)]
    sx = remote.make(SM.at[:, x, c, y], SM.at[:, x, c, y], place.at(x=1 - x))
    sy = remote.make(SM.at[:, :, c, y], SM.at[:, :, c, y], place.at(y=1 - y))
    sc = remote.make(SM.at[:, :, c], SM.at[:, :, c], place.at(c=1 - c))

    ga.step(0)
    for copy in sz:
        copy.start()
    xs.start()
    length = length_ref[0]
    seq_len = XF.shape[0] * local
    E[...] = key_structure(seq_len, length)
    ga.step(1)
    ga.step(2)
    for copy in sz:
        copy.wait_recv()
    sx.start()
    ga.step(3)
    ga.step(4)
    sx.wait_recv()
    sy.start()
    gi.step(0)
    gu.step(0)
    ga.step(5)
    ga.step(6)
    sy.wait_recv()
    sc.start()
    sc.wait_recv()
    ga.step(7)
    gi.step(1)
    gu.step(1)
    gi.step(2)
    put(WA, wa_hbm)

    tiles = SM[...].reshape(-1, 16, 128)
    pieces = tiles.shape[0]
    VEC[...] = spread_vectors(tiles, D // pieces, pieces)
    IB[...] = spread_vectors(tiles[:, 8:16, :], FF // pieces, pieces)
    put(VEC, vec_hbm)

    def wa(which):
        return WA[:, :, :, :, :, which * D : (which + 1) * D].reshape(D, D)

    Q[...] = ((dot_nn(XF[y], wa(0)) + VEC[0:1, :]).astype(bf16).astype(f32) * (HD**-0.5)).astype(bf16)
    put(Q, q_hbm)
    gu.step(2)
    gi.step(3)
    xs.wait_recv()
    put(XF, xf_hbm)
    for part in range(XF.shape[0]):
        rows = slice(part * local, (part + 1) * local)
        K[rows, :] = dot_nn(XF[part], wa(1)).astype(bf16)
    gu.step(3)
    gi.step(4)
    for part in range(XF.shape[0]):
        rows = slice(part * local, (part + 1) * local)
        values = (dot_nn(XF[part], wa(2)) + VEC[1:2, :]).astype(bf16)
        V[rows, :] = values
        VT[:, rows] = values.T
    put(K, k_hbm)
    put(V, v_hbm)

    position = y * local + lax.broadcasted_iota(jnp.int32, (1, local), 1)
    live = position < length

    def head_step(h, carry):
        pair = lax.div(h, 2)
        half = lax.rem(h, 2)
        lanes = ds128(pair, 128)
        own = pl.ds(pl.multiple_of(h * HD, HD), HD)
        left = jnp.concatenate([K[:, lanes], E[...]], axis=1)
        right = jnp.concatenate([head_lanes(Q[:, lanes], half), query_structure(compact_ref[h])], axis=1)
        for part in range(local // 256):
            cols = slice(part * 256, (part + 1) * 256)
            scores = dot_nt(left, right[cols, :])
            top = jnp.max(scores, axis=0, keepdims=True)
            exponent = jnp.exp(scores - top)
            total = jnp.sum(exponent, axis=0, keepdims=True)
            low = (exponent * (1.0 / total)).astype(bf16)
            AT[own, cols] = dot_nn(VT[own, :], low).astype(bf16)
            LSE[h, :, cols] = top + jnp.log(total)
            TOP[h, :, cols] = jnp.where(live[:, cols], top, neg_large)

        @pl.when(h == 0)
        def _():
            gu.step(4)

        @pl.when(h == 1)
        def _():
            gi.step(5)

        @pl.when(h == 2)
        def _():
            gu.step(5)

        @pl.when(h == 4)
        def _():
            gi.step(6)

        @pl.when(h == 6)
        def _():
            gu.step(6)

        return carry

    lax.fori_loop(0, H, head_step, 0)
    put(LSE, lse_hbm)
    put(TOP, top_hbm)
    A[...] = AT[...].T
    put(A, a_hbm)
    R1[...] = dot_nn(A[...], wa(3))

    def first_norm(k, carry):
        rows = ds128(k, 64)
        summed = XF[y, rows, :].astype(f32) + R1[rows, :] + VEC[2:3, :]
        R1[rows, :] = summed
        normal, _ = layer_norm_parts(summed)
        value = normal * VEC[3:4, :] + VEC[4:5, :]
        N1L[rows, :] = value.astype(bf16)
        R2[rows, :] = value + VEC[5:6, :]
        return carry

    lax.fori_loop(0, local // 64, first_norm, 0)
    put(R1, r1_hbm)
    gi.step(7)
    put(WI, wi_hbm)
    for part in range(3):
        cols = slice(part * 1024, (part + 1) * 1024)
        U[:, cols] = dot_nn(N1L[...], WI[:, :, :, :, :, cols].reshape(D, 1024)) + IB[0:1, cols]

    def activate(k, carry):
        rows = ds128(k, 16)
        u = U[rows, :]
        G[rows, :] = (u * (0.5 * (1.0 + lax.erf(u * np.float32(0.5**0.5))))).astype(bf16)
        return carry

    lax.fori_loop(0, local // 16, activate, 0)
    put(U, u_hbm)
    gu.step(7)
    put(WU, wu_hbm)
    R2[...] += dot_nn(G[...], WU[...].reshape(FF, D))

    def second_norm(k, carry):
        rows = ds128(k, 64)
        normal, _ = layer_norm_parts(R2[rows, :])
        OUT[rows, :] = (normal * VEC[6:7, :] + VEC[7:8, :]).astype(bf16)
        return carry

    lax.fori_loop(0, local // 64, second_norm, 0)
    put(R2, r2_hbm)
    put(OUT, out_hbm)
    remote.finish()
    for copy in outs:
        copy.wait()


def run_forward(nz, x, weights, small, compact, length):
    local = x.shape[0]
    wq, wk, wv, wo, wi, wu = weights
    grid = (nz, 2, 2, 2)
    rows, rows_u = wq.shape[0], wu.shape[0]
    seq = 2 * local
    outs = [
        ((local, D), bf16), ((local, D), f32), ((local, FF), f32), ((local, D), f32), ((local, D), bf16),
        ((local, D), bf16), ((seq, D), bf16), ((seq, D), bf16), ((2, local, D), bf16),
        ((H, 1, local), f32), ((H, 1, local), f32),
        ((*grid, rows, 4 * D), bf16), ((*grid, rows, FF), bf16), ((*grid, rows_u, D), bf16), ((16, D), f32),
    ]
    scratch = [
        ((*grid, rows, 4 * D), bf16), ((*grid, rows, FF), bf16), ((*grid, rows_u, D), bf16), ((*grid, 16, 128), bf16),
        ((2, local, D), bf16), ((local, D), bf16), ((seq, D), bf16), ((seq, D), bf16), ((D, seq), bf16),
        ((D, local), bf16), ((local, D), bf16), ((local, D), f32), ((local, D), f32), ((local, D), bf16),
        ((local, FF), f32), ((local, FF), bf16), ((8, 128), bf16), ((8, 128), f32), ((seq, 128), bf16),
        ((16, D), f32), ((8, FF), f32), ((H, 1, local), f32), ((H, 1, local), f32), ((local, D), bf16),
    ]
    copies = 1 + 3 * (2 * (nz - 1) + 6) + (nz - 1) + 3
    return pl.pallas_call(
        functools.partial(forward_kernel, nz, local),
        out_shape=[jax.ShapeDtypeStruct(*o) for o in outs],
        in_specs=[INSMEM, INVMEM] + [ANY] * 8,
        out_specs=[ANY] * len(outs),
        scratch_shapes=[pltpu.VMEM(*s) for s in scratch]
        + [
            pltpu.SemaphoreType.DMA((copies,)),
            pltpu.SemaphoreType.DMA((copies,)),
            pltpu.SemaphoreType.DMA((8,)),
            pltpu.SemaphoreType.DMA((len(outs),)),
        ],
        compiler_params=pltpu.CompilerParams(collective_id=1, has_side_effects=True, vmem_limit_bytes=60 << 20),
        name="gather_forward",
    )(length, compact, x, wq, wk, wv, wo, wi, wu, small)


def compact_mask(random_here, length, first_block):
    blocks = random_here.shape[0]
    query = (first_block + jnp.arange(blocks, dtype=jnp.int32))[None, :, None]
    lane = jnp.arange(128, dtype=jnp.int32)[None, None, :]
    last = (length - 1) // BLK
    ok = (jnp.abs(query - lane) <= 1) | (lane == 0) | (lane == last) | (query == 0) | (query == last)
    heads = jnp.transpose(random_here, (1, 0, 2))
    for k in range(heads.shape[2]):
        ok = ok | (heads[:, :, k : k + 1] == lane)
    shown = jnp.where(lane < NB, jnp.where(ok, 0.0, neg_large), jnp.where(lane == NB, neg_large, 0.0))
    return shown.astype(f32)


def pack_small(vectors, wide):
    rows = [jnp.pad(v, (0, 128 - v.shape[0])) for v in vectors] + [jnp.pad(wide, (0, 128 - wide.shape[0]))]
    rows += [jnp.zeros((128,), bf16)] * (16 - len(rows))
    return jnp.stack(rows)


def back_pair(pair, local, compact_ref, Q, K, V, KT, DA, LSE, E, PB, DS, DQT, DK, DV):
    lanes = ds128(pair, 128)
    q_pair, a_pair, k_pair, v_pair = Q[:, lanes], DA[:, lanes], K[:, lanes], V[:, lanes]
    left = jnp.concatenate([k_pair, E[...]], axis=1)
    q_heads = [head_lanes(q_pair, half) for half in (0, 1)]
    a_heads = [head_lanes(a_pair, half) for half in (0, 1)]
    for half in (0, 1):
        h = pair * 2 + half
        own = pl.ds(pl.multiple_of(h * HD, HD), HD)
        right = jnp.concatenate([q_heads[half], query_structure(compact_ref[h])], axis=1)
        for part in range(local // 256):
            cols = slice(part * 256, (part + 1) * 256)
            place = slice(half * local + part * 256, half * local + (part + 1) * 256)
            prob = jnp.exp(dot_nt(left, right[cols, :]) - LSE[h, :, cols])
            PB[:, place] = prob.astype(bf16)
            dprob = dot_nt(v_pair, a_heads[half][cols, :])
            inner = jnp.sum(prob * dprob, axis=0, keepdims=True)
            low = (prob * (dprob - inner)).astype(bf16)
            DS[:, place] = low
            DQT[own, cols] = (dot_nn(KT[own, :], low) * (HD**-0.5)).astype(bf16)
    DK[:, lanes] = dot_nn(DS[...], jnp.concatenate(q_heads, axis=0)).astype(bf16)
    DV[:, lanes] = dot_nn(PB[...], jnp.concatenate(a_heads, axis=0)).astype(bf16)


def attend_back_kernel(local, length_ref, compact_ref, Q, K, V, DA, LSE, DQ, DK, DV, E, KT, PB, DS, DQT):
    E[...] = key_structure(K.shape[0], length_ref[0])
    KT[...] = K[...].T

    def step(pair, carry):
        back_pair(pair, local, compact_ref, Q, K, V, KT, DA, LSE, E, PB, DS, DQT, DK, DV)
        return carry

    lax.fori_loop(0, H // 2, step, 0)
    DQ[...] = DQT[...].T


def run_attend_back(q, k, v, da, lse, compact, length):
    local, seq = q.shape[0], k.shape[0]
    outs = [((local, D), bf16), ((seq, D), bf16), ((seq, D), bf16)]
    scratch = [((seq, 128), bf16), ((D, seq), bf16), ((seq, 2 * local), bf16), ((seq, 2 * local), bf16), ((D, local), bf16)]
    return pl.pallas_call(
        functools.partial(attend_back_kernel, local),
        out_shape=[jax.ShapeDtypeStruct(*o) for o in outs],
        in_specs=[INSMEM] + [INVMEM] * 6,
        out_specs=[INVMEM] * 3,
        scratch_shapes=[pltpu.VMEM(*s) for s in scratch],
        compiler_params=pltpu.CompilerParams(vmem_limit_bytes=60 << 20),
        name="attend_back",
    )(length, compact, q, k, v, da, lse)


class Scatter:
    def __init__(self, remote, place, g, bufs, out, width):
        rc, ra1, ra2, raz, rb1, rbz, rb2 = bufs
        z, x, c, y = place.z, place.x, place.c, place.y
        half = width // 2
        a, b = slice(0, half), slice(half, width)
        self.place, self.g, self.bufs, self.out, self.a, self.b = place, g, bufs, out, a, b
        self.core = remote.make(g.at[:, :, 1 - c], rc, place.at(c=1 - c))
        self.a1 = remote.make(g.at[:, :, c, 1 - y, :, a], ra1, place.at(y=1 - y))
        self.b1 = remote.make(g.at[:, 1 - x, c, :, :, b], rb1, place.at(x=1 - x))
        self.a2 = remote.make(g.at[:, 1 - x, c, y, :, a], ra2, place.at(x=1 - x))
        self.bz, self.az = [], []
        for k in range(1, place.nz):
            zk = place.z_off(k)
            self.bz.append(remote.make(g.at[zk, x, c, :, :, b], rbz.at[k - 1], place.at(z=zk)))
            self.az.append(remote.make(g.at[zk, x, c, y, :, a], raz.at[k - 1], place.at(z=zk)))
        self.b2 = remote.make(g.at[z, x, c, 1 - y, :, b], rb2, place.at(y=1 - y))

    def step(self, n):
        rc, ra1, ra2, raz, rb1, rbz, rb2 = self.bufs
        place, g, a, b = self.place, self.g, self.a, self.b
        z, x, c, y = place.z, place.x, place.c, place.y
        if n == 0:
            self.core.start()
        elif n == 1:
            self.core.wait_recv()

            def add_core(k, carry):
                zz, xx = lax.div(k, 2), lax.rem(k, 2)
                for yy in range(2):
                    g[zz, xx, c, yy] = (g[zz, xx, c, yy].astype(f32) + rc[zz, xx, yy].astype(f32)).astype(bf16)
                return carry

            lax.fori_loop(0, place.nz * 2, add_core, 0)
            self.a1.start()
            self.b1.start()
        elif n == 2:
            self.a1.wait_recv()

            def add_a1(k, carry):
                zz, xx = lax.div(k, 2), lax.rem(k, 2)
                g[zz, xx, c, y, :, a] = (g[zz, xx, c, y, :, a].astype(f32) + ra1[zz, xx].astype(f32)).astype(bf16)
                return carry

            lax.fori_loop(0, place.nz * 2, add_a1, 0)
            self.a2.start()
        elif n == 3:
            self.b1.wait_recv()

            def add_b1(k, carry):
                zz, yy = lax.div(k, 2), lax.rem(k, 2)
                g[zz, x, c, yy, :, b] = (g[zz, x, c, yy, :, b].astype(f32) + rb1[zz, yy].astype(f32)).astype(bf16)
                return carry

            lax.fori_loop(0, place.nz * 2, add_b1, 0)
            for copy in self.bz:
                copy.start()
        elif n == 4:
            self.a2.wait_recv()
            for zz in range(place.nz):
                g[zz, x, c, y, :, a] = (g[zz, x, c, y, :, a].astype(f32) + ra2[zz].astype(f32)).astype(bf16)
            for copy in self.az:
                copy.start()
        elif n == 5:
            for copy in self.bz:
                copy.wait_recv()
            for yy in range(2):
                total = g[z, x, c, yy, :, b].astype(f32)
                for k in range(place.nz - 1):
                    total = total + rbz[k, yy].astype(f32)
                g[z, x, c, yy, :, b] = total.astype(bf16)
            self.b2.start()
        elif n == 6:
            for copy in self.az:
                copy.wait_recv()
            total = g[z, x, c, y, :, a].astype(f32)
            for k in range(place.nz - 1):
                total = total + raz[k].astype(f32)
            self.out[:, a] = total
        elif n == 7:
            self.b2.wait_recv()
            self.out[:, b] = g[z, x, c, y, :, b].astype(f32) + rb2[...].astype(f32)


def scatter_buffers(nz, rows, width):
    half = width // 2
    return [
        ((nz, 2, 2, rows, width), bf16), ((nz, 2, rows, half), bf16), ((nz, rows, half), bf16), ((nz - 1, rows, half), bf16),
        ((nz, 2, rows, half), bf16), ((nz - 1, 2, rows, half), bf16), ((rows, half), bf16),
    ]


class SmallSums:
    def __init__(self, remote, place, t, bufs, top, tops):
        rc, ry, rx, rz = bufs
        z, x, c, y = place.z, place.x, place.c, place.y
        self.place, self.t, self.bufs, self.top, self.tops = place, t, bufs, top, tops
        self.stages = [
            [remote.make(t.at[:, :, 1 - c], rc, place.at(c=1 - c))],
            [remote.make(t.at[:, :, c, 1 - y], ry, place.at(y=1 - y))],
            [remote.make(t.at[:, 1 - x, c, y], rx, place.at(x=1 - x))],
            [
                remote.make(t.at[place.z_off(k), x, c, y], rz.at[k - 1], place.at(z=place.z_off(k)))
                for k in range(1, place.nz)
            ],
        ]
        to = [[place.at(c=1 - c)], [place.at(y=1 - y)], [place.at(x=1 - x)]]
        to.append([place.at(z=place.z_off(k)) for k in range(1, place.nz)])
        self.top_stages, slot = [], 0
        for n, peers in enumerate(to):
            made = []
            for peer in peers:
                made.append((remote.make(top.at[n], tops.at[slot], peer), slot))
                slot += 1
            self.top_stages.append(made)

    def start(self, n):
        for copy in self.stages[n]:
            copy.start()
        for copy, _ in self.top_stages[n]:
            copy.start()

    def take(self, n):
        place, t = self.place, self.t
        rc, ry, rx, rz = self.bufs
        z, x, c, y = place.z, place.x, place.c, place.y
        for copy in self.stages[n]:
            copy.wait_recv()
        best = self.top[n]
        for copy, slot in self.top_stages[n]:
            copy.wait_recv()
            best = jnp.maximum(best, self.tops[slot])
        self.top[n + 1] = best
        if n == 0:
            t[:, :, c] = t[:, :, c] + rc[...]
        elif n == 1:
            t[:, :, c, y] = t[:, :, c, y] + ry[...]
        elif n == 2:
            t[:, x, c, y] = t[:, x, c, y] + rx[...]
        else:
            total = t[z, x, c, y]
            for k in range(place.nz - 1):
                total = total + rz[k]
            t[z, x, c, y] = total


def small_buffers(nz):
    return [((nz, 2, 2, 16, 128), f32), ((nz, 2, 16, 128), f32), ((nz, 16, 128), f32), ((nz - 1, 16, 128), f32)]


def scatter_kernel(nz, widths, da_hbm, di_hbm, du_hbm, sm_hbm, top_hbm, oa, oi, ou, osm, otop, *rest):
    place = Place(nz)
    ga, gi, gu, t, top, tops = rest[:6]
    bufs = [rest[6 + 7 * k : 13 + 7 * k] for k in range(3)]
    sbufs = rest[27:31]
    send_sems, recv_sems, local_sems = rest[31:]
    loads = [
        pltpu.make_async_copy(src, dst, local_sems.at[k])
        for k, (src, dst) in enumerate([(sm_hbm, t), (top_hbm, top.at[0]), (du_hbm, gu), (di_hbm, gi), (da_hbm, ga)])
    ]
    for copy in loads:
        copy.start()
    entry_barrier(place)
    remote = Remote(send_sems, recv_sems)
    small = SmallSums(remote, place, t, sbufs, top, tops)
    parts = [
        Scatter(remote, place, g, bufs[k], out, width)
        for k, (g, out, width) in enumerate([(gu, ou, widths[2]), (gi, oi, widths[1]), (ga, oa, widths[0])])
    ]
    loads[0].wait()
    loads[1].wait()
    small.start(0)
    for n, part in enumerate(parts):
        loads[2 + n].wait()
        part.step(0)
    small.take(0)
    small.start(1)
    for n in range(1, 8):
        for part in parts:
            part.step(n)
        if n < 4:
            small.take(n)
            if n < 3:
                small.start(n + 1)
    osm[...] = t[place.z, place.x, place.c, place.y]
    otop[...] = top[4]
    remote.finish()


def run_scatter(nz, da, di, du, sm, top):
    grid = (nz, 2, 2, 2)
    shapes = [a.shape[-2:] for a in (da, di, du)]
    outs = [(s, f32) for s in shapes] + [((16, 128), f32), ((16, 128), f32)]
    scratch = [(a.shape, bf16) for a in (da, di, du)] + [(sm.shape, f32), ((5, 16, 128), f32), ((3 + nz - 1, 16, 128), f32)]
    for s in (shapes[2], shapes[1], shapes[0]):
        scratch += scatter_buffers(nz, *s)
    scratch += small_buffers(nz)
    copies = 3 * (2 * (nz - 1) + 5) + 2 * (3 + nz - 1)
    return pl.pallas_call(
        functools.partial(scatter_kernel, nz, [s[1] for s in shapes]),
        out_shape=[jax.ShapeDtypeStruct(*o) for o in outs],
        in_specs=[ANY] * 5,
        out_specs=[INVMEM] * 5,
        scratch_shapes=[pltpu.VMEM(*s) for s in scratch]
        + [pltpu.SemaphoreType.DMA((copies,)), pltpu.SemaphoreType.DMA((copies,)), pltpu.SemaphoreType.DMA((5,))],
        compiler_params=pltpu.CompilerParams(collective_id=2, has_side_effects=True, vmem_limit_bytes=60 << 20),
        name="scatter_gradients",
    )(da, di, du, sm, top)


def layer_norm(row_values, gain_vector, shift_vector):
    centre = row_values - jnp.mean(row_values, axis=-1, keepdims=True)
    spread = jnp.mean(centre * centre, axis=-1, keepdims=True)
    return centre * lax.rsqrt(spread + norm_eps) * gain_vector + shift_vector


def gelu_exact(values):
    return jax.nn.gelu(values, approximate=False)


def column_sums(values):
    return jnp.sum(values.astype(f32), axis=0)


def clip_outputs(logit_maxima, threshold, query_weight, query_bias, key_weight, device_rank):
    clip_limit = threshold.astype(f32)[0] * 0.01
    factors = jnp.sqrt(clip_limit / jnp.maximum(logit_maxima, clip_limit))
    column_scale = jnp.repeat(factors, HD)
    query_clipped = (query_weight.astype(f32) * column_scale[None, :]).astype(bf16)
    key_clipped = (key_weight.astype(f32) * column_scale[None, :]).astype(bf16)
    bias_count = query_bias.shape[0]
    bias_heads = (device_rank * bias_count + jnp.arange(bias_count)) // HD
    bias_scale = jnp.sum(jnp.where(bias_heads[:, None] == jnp.arange(H)[None, :], factors[None, :], 0.0), axis=1)
    return query_clipped, (query_bias.astype(f32) * bias_scale).astype(bf16), key_clipped


def tiles_of(vectors, wide, pieces, grid):
    rows = [jnp.pad(v.reshape(pieces, -1), ((0, 0), (0, 128 - v.shape[0] // pieces))) for v in vectors]
    rows.append(jnp.pad(wide.reshape(pieces, -1), ((0, 0), (0, 128 - wide.shape[0] // pieces))))
    rows += [jnp.zeros((pieces, 128), f32)] * (16 - len(rows))
    return jnp.stack(rows, axis=1).reshape(*grid, 16, 128)


def fast_shards(
    nz,
    inputs, cotangent, query_weight, query_bias, key_weight, value_weight, value_bias, output_weight, output_bias,
    first_gain, first_shift, inner_weight, inner_bias, outer_weight, outer_bias, second_gain, second_shift,
    lengths, random_blocks, threshold,
):
    local = inputs.shape[1]
    grid = (nz, 2, 2, 2)
    pieces = nz * 8
    rows, rows_u = query_weight.shape[0], outer_weight.shape[0]
    y = lax.axis_index("ctx")
    blocks = local // BLK
    first_block = y * blocks
    random_here = lax.dynamic_slice_in_dim(random_blocks[0], first_block, blocks, 0)
    compact = compact_mask(random_here, lengths[0], first_block)
    small = pack_small(
        [query_bias, value_bias, output_bias, first_gain, first_shift, outer_bias, second_gain, second_shift], inner_bias
    )
    x = inputs[0]
    weights = (query_weight, key_weight, value_weight, output_weight, inner_weight, outer_weight)
    (
        output, first_sum, pre_act, second_sum, attended, q, k, v, x_both, lse, tops, wa, wi, wu, vectors
    ) = run_forward(nz, x, weights, small, compact, lengths)
    wa, wi, wu = wa.reshape(D, 4 * D), wi.reshape(D, FF), wu.reshape(FF, D)
    full_query, full_key, full_value, full_out = (wa[:, n * D : (n + 1) * D] for n in range(4))
    gain_one, shift_one, gain_two, shift_two = vectors[3], vectors[4], vectors[6], vectors[7]
    normed_low = layer_norm(first_sum, gain_one, shift_one).astype(bf16)
    activated = gelu_exact(pre_act).astype(bf16)
    live = (y * local + jnp.arange(local)) < lengths[0]
    cot_rows = jnp.where(live[:, None], cotangent[0].astype(f32), 0.0)
    second_pull = jax.vjp(layer_norm, second_sum, gain_two, shift_two)[1]
    grad_second, second_gain_grad, second_shift_grad = second_pull(cot_rows)
    grad_outer_low = grad_second.astype(bf16)
    outer_bias_grad = column_sums(grad_outer_low)
    outer_weight_grad = dot_tn(activated, grad_outer_low)
    grad_activated = dot_nt(grad_outer_low, wu)
    grad_pre_low = jax.vjp(gelu_exact, pre_act)[1](grad_activated)[0].astype(bf16)
    inner_bias_grad = column_sums(grad_pre_low)
    inner_weight_grad = dot_tn(normed_low, grad_pre_low)
    grad_normed = grad_second + dot_nt(grad_pre_low, wi)
    first_pull = jax.vjp(layer_norm, first_sum, gain_one, shift_one)[1]
    grad_first, first_gain_grad, first_shift_grad = first_pull(grad_normed)
    grad_proj_low = grad_first.astype(bf16)
    output_bias_grad = column_sums(grad_proj_low)
    output_weight_grad = dot_tn(attended, grad_proj_low)
    grad_attended = dot_nt(grad_proj_low, full_out).astype(bf16)
    dq, dk, dv = run_attend_back(q, k, v, grad_attended, lse, compact, lengths)
    x_rows = x_both.reshape(2 * local, D)
    query_weight_grad = dot_tn(x, dq)
    query_bias_grad = column_sums(dq)
    key_weight_grad = dot_tn(x_rows, dk)
    value_weight_grad = dot_tn(x_rows, dv)
    value_bias_grad = column_sums(dv)
    through = dot_nt(dk, full_key) + dot_nt(dv, full_value)
    own = lax.dynamic_slice_in_dim(through, y * local, local, 0)
    other = lax.dynamic_slice_in_dim(through, (1 - y) * local, local, 0).astype(bf16)
    received = lax.ppermute(other, "ctx", [(0, 1), (1, 0)]).astype(f32)
    input_grad = grad_first + dot_nt(dq, full_query) + own + received
    da = jnp.concatenate(
        [query_weight_grad, key_weight_grad, value_weight_grad, output_weight_grad], axis=1
    ).astype(bf16).reshape(*grid, rows, 4 * D)
    di = inner_weight_grad.astype(bf16).reshape(*grid, rows, FF)
    du = outer_weight_grad.astype(bf16).reshape(*grid, rows_u, D)
    sm = tiles_of(
        [query_bias_grad, value_bias_grad, output_bias_grad, first_gain_grad, first_shift_grad, outer_bias_grad,
         second_gain_grad, second_shift_grad], inner_bias_grad, pieces, grid,
    )
    top_here = jnp.broadcast_to(jnp.pad(jnp.max(tops[:, 0, :], axis=1), (0, 4))[:, None], (16, 128))
    ga, gi, gu, gs, top = run_scatter(nz, da, di, du, sm, top_here)
    logit_maxima = top[:H, 0]
    rank = lax.axis_index("dp") * 2 + y
    query_clipped, bias_clipped, key_clipped = clip_outputs(
        logit_maxima, threshold, query_weight, query_bias, key_weight, rank
    )
    vec = [gs[n, :rows] for n in range(8)]
    return (
        output[None], input_grad[None],
        ga[:, :D], vec[0], ga[:, D : 2 * D], ga[:, 2 * D : 3 * D], vec[1], ga[:, 3 * D :], vec[2], vec[3], vec[4],
        gi, gs[8, : FF // pieces], gu, vec[5], vec[6], vec[7],
        query_clipped, bias_clipped, key_clipped, logit_maxima,
    )


def general_shards(
    inputs, cotangent, query_weight, query_bias, key_weight, value_weight, value_bias, output_weight, output_bias,
    first_gain, first_shift, inner_weight, inner_bias, outer_weight, outer_bias, second_gain, second_shift,
    lengths, random_blocks, threshold,
):
    both = ("dp", "ctx")
    shards = (
        query_weight, query_bias, key_weight, value_weight, value_bias, output_weight, output_bias, first_gain, first_shift,
        inner_weight, inner_bias, outer_weight, outer_bias, second_gain, second_shift,
    )
    wq, bq, wk, wv, bv, wo, bo, g1, s1, wi, bi, wu, bu, g2, s2 = (lax.all_gather(w, both, axis=0, tiled=True) for w in shards)
    bq, bv, bo, g1, s1, bi, bu, g2, s2 = (v.astype(f32) for v in (bq, bv, bo, g1, s1, bi, bu, g2, s2))
    seqs, local, _ = inputs.shape
    blocks = local // BLK
    y = lax.axis_index("ctx")
    first_block = y * blocks
    scale = HD**-0.5
    outs = []
    sums = None
    top = jnp.full((H,), neg_large, f32)
    for s in range(seqs):
        x, length = inputs[s], lengths[s]
        random_here = lax.dynamic_slice_in_dim(random_blocks[s], first_block, blocks, 0)
        mask = compact_mask(random_here, length, first_block)[:, :, :NB]
        mask = jnp.repeat(jnp.repeat(mask, BLK, axis=1), BLK, axis=2)
        seen = jnp.arange(NB * BLK) < length
        mask = jnp.where(seen[None, None, :], mask, neg_large)
        live = (y * local + jnp.arange(local)) < length
        q = (dot_nn(x, wq) + bq).astype(bf16)
        k = lax.all_gather(dot_nn(x, wk).astype(bf16), "ctx", axis=0, tiled=True)
        v = lax.all_gather((dot_nn(x, wv) + bv).astype(bf16), "ctx", axis=0, tiled=True)
        qh, kh, vh = (a.reshape(-1, H, HD) for a in (q, k, v))
        raw = jnp.einsum("qhd,khd->hqk", qh, kh, preferred_element_type=f32) * scale + mask
        row_top = jnp.max(raw, axis=-1, keepdims=True)
        top = jnp.maximum(top, jnp.max(jnp.where(live[None, :, None], row_top, neg_large), axis=(1, 2)))
        exponent = jnp.exp(raw - row_top)
        prob = exponent / jnp.sum(exponent, axis=-1, keepdims=True)
        low = prob.astype(bf16)
        attended = jnp.einsum("hqk,khd->qhd", low, vh, preferred_element_type=f32).reshape(local, D).astype(bf16)
        first_sum = x.astype(f32) + dot_nn(attended, wo) + bo
        normed = layer_norm(first_sum, g1, s1)
        normed_low = normed.astype(bf16)
        pre_act = dot_nn(normed_low, wi) + bi
        activated = gelu_exact(pre_act).astype(bf16)
        second_sum = normed + dot_nn(activated, wu) + bu
        output = layer_norm(second_sum, g2, s2).astype(bf16)
        cot = jnp.where(live[:, None], cotangent[s].astype(f32), 0.0)
        grad_second, g2_grad, s2_grad = jax.vjp(layer_norm, second_sum, g2, s2)[1](cot)
        dm = grad_second.astype(bf16)
        du = jax.vjp(gelu_exact, pre_act)[1](dot_nt(dm, wu))[0].astype(bf16)
        grad_normed = grad_second + dot_nt(du, wi)
        grad_first, g1_grad, s1_grad = jax.vjp(layer_norm, first_sum, g1, s1)[1](grad_normed)
        dp = grad_first.astype(bf16)
        da = dot_nt(dp, wo).astype(bf16).reshape(local, H, HD)
        dprob = jnp.einsum("qhd,khd->hqk", da, vh, preferred_element_type=f32)
        ds = (prob * (dprob - jnp.sum(prob * dprob, axis=-1, keepdims=True))).astype(bf16)
        dq = (jnp.einsum("hqk,khd->qhd", ds, kh, preferred_element_type=f32) * scale).reshape(local, D).astype(bf16)
        dk = (jnp.einsum("hqk,qhd->khd", ds, qh, preferred_element_type=f32) * scale).reshape(-1, D)
        dv = jnp.einsum("hqk,qhd->khd", low, da, preferred_element_type=f32).reshape(-1, D)
        dk, dv = (lax.psum_scatter(a.astype(bf16), "ctx", scatter_dimension=0, tiled=True).astype(bf16) for a in (dk, dv))
        input_grad = grad_first + dot_nt(dq, wq) + dot_nt(dk, wk) + dot_nt(dv, wv)
        outs.append((output, input_grad))
        here = (
            dot_tn(x, dq), column_sums(dq), dot_tn(x, dk), dot_tn(x, dv), column_sums(dv), dot_tn(attended, dp),
            column_sums(dp), g1_grad, s1_grad, dot_tn(normed_low, du), column_sums(du), dot_tn(activated, dm),
            column_sums(dm), g2_grad, s2_grad,
        )
        sums = here if sums is None else tuple(a + b for a, b in zip(sums, here))
    grads = tuple(lax.psum_scatter(g, both, scatter_dimension=0, tiled=True) for g in sums)
    logit_maxima = lax.pmax(top, both)
    rank = lax.axis_index(both)
    clipped = clip_outputs(logit_maxima, threshold, query_weight, query_bias, key_weight, rank)
    return (jnp.stack([o for o, _ in outs]), jnp.stack([g for _, g in outs]), *grads, *clipped, logit_maxima)


def solution(mesh):
    both = P(("dp", "ctx"))
    rows = P(("dp", "ctx"), None)
    tokens = P("dp", "ctx", None)
    in_specs = (
        tokens, tokens, rows, both, rows, rows, both, rows, both, both, both, rows, both, rows, both, both, both,
        P("dp"), P("dp", None, None, None), P(),
    )
    out_specs = (
        tokens, tokens, rows, both, rows, rows, both, rows, both, both, both, rows, both, rows, both, both, both,
        rows, both, rows, P(),
    )
    dp, ctx = mesh.shape["dp"], mesh.shape["ctx"]
    pieces = dp * ctx
    fits = ctx == 2 and dp % 4 == 0 and D % (8 * pieces) == 0 and FF // pieces <= 128

    def step(*args):
        if fits and args[0].shape[0] == 1:
            return fast_shards(dp // 4, *args)
        return general_shards(*args)

    return jax.shard_map(step, mesh=mesh, in_specs=in_specs, out_specs=out_specs, check_vma=False)
```

time: 1560 us -> 376 us (0.24)
  waiting for transfers between devices: 781 us -> 0.01 us
  other arithmetic: 309 us -> 19.2 us
  Pallas kernels: 0 us -> 258 us
  matrix products: 191 us -> 66.8 us
  blocking collectives: 121 us -> 0 us
  local copies, waits for them, and re-layouts: 133 us -> 23.5 us
    reduce_scatter x5 -> x0, waiting for transfers between devices: 360 us -> none  [the longest x1 142 us: shards(): lax.psum_scatter(outer_weight_grad, ('dp', 'ctx'), scatter_dimension=0, t...]
    pallas_call x0 -> x3, Pallas kernels: none -> 258 us  [the longest x1 115 us: run_scatter(): pl.pallas_call(functools.partial(scatter_kernel, nz, [s[1] for s in shape...]
    scatter-add x2 -> x0, other arithmetic: 244 us -> none  [attend_back(): jnp.zeros((NB, H, BLK, HD), jnp.float32).at[safe_ids, head_ids]]
    unnamed x19 -> x0, waiting for transfers between devices: 213 us -> none
    all_gather x8 -> x0, waiting for transfers between devices: 209 us -> none  [the longest x1 58.4 us: shards(): lax.all_gather(key_weight, ('dp', 'ctx'), axis=0, tiled=True)]
    dot_general x28 -> x12, matrix products: 188 us -> 66.8 us  [the longest x6 41.1 us: dot_nt(): lax.dot_general(a, b, (((1,), (1,)), ((), ())), preferred_element_type=f32)]
    unnamed x2 -> x0, blocking collectives: 80.8 us -> none
    pmax x1 -> x0, blocking collectives: 39.9 us -> none  [shards(): logit_maxima = lax.pmax(top_local, ('dp', 'ctx'))]
  transfers between devices with their start and end apart: 16 -> 1, of which waited for: 12 -> 0; matrix products, arithmetic and copies ran while one was open for 26% -> 12% of each run, Pallas kernels for 0% -> 31%
where the time goes in v1:
time: 376 us; the launch traced here: 372 us
  Pallas kernels  258 us (69%)
  matrix products  66.8 us (18%)
  local copies, waits for them, and re-layouts  23.5 us (6%)
  other arithmetic  19.2 us (5%)
    pallas_call x1, Pallas kernels, run_scatter(): pl.pallas_call(functools.partial(scatter_kernel, nz, [s[1] for s in shape...  115 us
    pallas_call x1, Pallas kernels, run_forward(): pl.pallas_call(functools.partial(forward_kernel, nz, local), out_shape=[j...  115 us
    dot_general x6, matrix products, dot_nt(): lax.dot_general(a, b, (((1,), (1,)), ((), ())), preferred_element_type=f32)  41.1 us
    pallas_call x1, Pallas kernels, run_attend_back(): pl.pallas_call(functools.partial(attend_back_kernel, local), out_shape=[j...  28.3 us
    dot_general x6, matrix products, dot_tn(): lax.dot_general(a, b, (((0,), (0,)), ((), ())), preferred_element_type=f32)  25.7 us
  transfers between devices with their start and end apart: 1, of which 0 were waited for; matrix products, arithmetic and copies ran while one was open for 12% of the time, Pallas kernels for 31%

profile of v1, /device:TPU:0, one launch (start us, length us, event | category | flops | bytes accessed | tf_op | source)
XLA Modules:
  0.0 371.9 jit_solution(5942513965941125426)
XLA Ops:
  1.9 0.7 pad_bitcast_fusion.8
  2.6 0.7 pad_bitcast_fusion
  3.2 0.7 pad_bitcast_fusion.2
  3.9 0.7 pad_bitcast_fusion.4
  4.6 0.7 pad_bitcast_fusion.6
  5.3 0.7 select_select_fusion.compact_ref
  6.1 1.2 stack.83.small
  7.3 114.9 %gather_forward.1 = (bf16[512,768]{1,0:T(8,128)(2,1)}, f32[512,768]{1,0:T(8,128)}, f32[512,3072]{1,0:T(8,128)}, f32[512,768]{1,0:T(8,128)}, bf16[512,768]{1,0:T(...) custom-call(s32[1]{0:T(128)} %copy.61.length_ref, ...), custom_call_target="tpu_custom_call" | custom-call | tf_op jit(solution)/shard_map/gather_forward/pallas_call | solution.py:400
  122.2 1.7 reduce_sum.156
  123.9 1.7 multiply_reduce_fusion.3
  125.6 0.9 slice_reduce_fusion.1
  126.5 2.0 fusion.17
  128.6 2.9 fusion.46
  131.7 0.3 multiply_reduce_fusion.2
  132.0 0.9 copy-done.4
  133.1 19.9 %convert_reduce_fusion = (f32[3072]{0:T(1024)S(1)}, bf16[512,3072]{1,0:T(8,128)(2,1)S(1)}, f32[512,3072]{1,0:T(8,128)}) fusion(f32[512,3072]{1,0:T(8,128)} %get-tuple-element.47, bf16[512,768]{1,0:T(8,128)(2,1)S(1)} %get-tuple-element.80, bf16[3072,768]{1,0:T(8,128)(2,1)} %bitcast.139), kind=kOutput, calls=%fused_computation.2 | convolution fusion | flops 2532307968 | bytes 21245952 | tf_op jit(solution)/shard_map/dot_general | solution.py:34
  153.1 3.2 multiply_reduce_fusion
  156.3 0.7 fusion.45
  157.0 0.2 convert_reduce_fusion.3
  157.2 0.9 copy-done.13
  158.1 3.0 convolution_convert_fusion.4.DA
  161.0 28.3 %attend_back.1 = (bf16[512,768]{1,0:T(8,128)(2,1)}, bf16[1024,768]{1,0:T(8,128)(2,1)}, bf16[1024,768]{1,0:T(8,128)(2,1)}) custom-call(s32[1]{0:T(128)} %copy.61.length_ref, f32[12,8,128]{2,1,0:T(8,128)} %select_select_fusion.compact_ref, bf16[512,768]{1,0:T(8,128)(2,1)} %get-tuple-element.51.Q, bf16[1024,768]{1,0:T(8,128)(2,1)} %get-tuple-element.52.K, ...), custom_call_target="tpu_custom_call" | custom-call | tf_op jit(solution)/shard_map/attend_back/pallas_call | solution.py:476
  189.4 4.9 %fusion.25 = f32[1024,768]{1,0:T(8,128)} fusion(bf16[1024,768]{1,0:T(8,128)(2,1)} %get-tuple-element.57, bf16[768,3072]{1,0:T(8,128)(2,1)} %bitcast.121), kind=kOutput, calls=%fused_computation.57 | convolution fusion | flops 1207959552 | bytes 5898240 | tf_op jit(solution)/shard_map/dot_general | solution.py:34
  194.3 5.9 %convolution_add_fusion = f32[1024,768]{1,0:T(8,128)} fusion(f32[1024,768]{1,0:T(8,128)} %fusion.25, bf16[1024,768]{1,0:T(8,128)(2,1)} %get-tuple-element.58, bf16[768,3072]{1,0:T(8,128)(2,1)} %bitcast.122), kind=kOutput, calls=%fused_computation.25 | convolution fusion | flops 1208745984 | bytes 9043968 | tf_op jit(solution)/shard_map/dot_general | solution.py:34
  200.2 2.4 dynamic-slice_convert_fusion
  202.6 1.5 collective-permute-start
  204.1 1.7 convert_reduce_fusion.1
  205.8 2.6 copy.55
  208.4 4.5 %fusion.18 = bf16[4,2,2,2,24,768]{5,4,3,2,1,0:T(8,128)(2,1)} fusion(bf16[4,2,2,2,24,1024]{5,4,3,2,1,0:T(8,128)(2,1)} %bitcast.116, bf16[1024,768]{1,0:T(8,128)(2,1)} %get-tuple-element.57), kind=kOutput, calls=%fused_computation.48 | convolution fusion | flops 1208549376 | bytes 4325376 | tf_op jit(solution)/shard_map/dot_general | solution.py:38
  212.9 2.5 fusion.21
  215.5 1.9 convolution_convert_fusion.3
  218.3 10.2 %convolution_convert_fusion = bf16[3072,768]{1,0:T(8,128)(2,1)} fusion(bf16[512,768]{1,0:T(8,128)(2,1)} %copy-done.8, f32[512,3072]{1,0:T(8,128)} %get-tuple-element.78, f32[512,3072]{1,0:T(8,128)} %get-tuple-element.47), kind=kOutput, calls=%fused_computation.18 | convolution fusion | flops 2422996992 | bytes 18087936 | tf_op jit(solution)/shard_map/dot_general | solution.py:38
  228.5 4.8 %convolution_convert_fusion.1 = bf16[768,3072]{1,0:T(8,128)(2,1)} fusion(bf16[512,3072]{1,0:T(8,128)(2,1)S(1)} %copy-done.24, f32[512,768]{1,0:T(8,128)S(1)} %copy-done.3, f32[768]{0:T(1024)S(1)} %get-tuple-element.73, f32[512]{0:T(512)S(1)} %fusion.41, f32[512]{0:T(512)S(1)} %broadcast_multiply_fusion, f32[768]{0:T(1024)S(1)} %get-tuple-element.74), kind=kOutput, calls=%fused_computation.19 | convolution fusion | flops 2420244480 | bytes 9447424 | tf_op jit(solution)/shard_map/dot_general | solution.py:38
  233.3 1.8 convolution_convert_fusion.2
  235.4 5.2 %pad_maximum_fusion.da_hbm = bf16[4,2,2,2,24,3072]{5,4,3,2,1,0:T(8,128)(2,1)} fusion(bf16[4,2,2,2,24,768]{5,4,3,2,1,0:T(8,128)(2,1)} %bitcast.119, bf16[4,2,2,2,24,768]{5,4,3,2,1,0:T(8,128)(2,1)} %fusion.21, bf16[4,2,2,2,24,768]{5,4,3,2,1,0:T(8,128)(2,1)S(1)} %copy-done.10, bf16[4,2,2,2,24,768]{5,4,3,2,1,0:T(8,128)(2,1)} %bitcast.118), kind=kLoop, calls=%fused_computation.20 | loop fusion | flops 18874368 | bytes 9437184 | tf_op jit(solution)/shard_map/concatenate | solution.py:788
  240.6 1.6 stack.95.sm_hbm
  242.2 0.7 broadcast_in_dim.109.top_hbm
  242.8 115.0 %scatter_gradients.1 = (f32[24,3072]{1,0:T(8,128)}, f32[24,3072]{1,0:T(8,128)}, f32[96,768]{1,0:T(8,128)}, f32[16,128]{1,0:T(8,128)}, f32[16,128]{1,0:T(8,128)}) custom-call(bf16[4,2,2,2,24,3072]{5,4,3,2,1,0:T(8,128)(2,1)} %pad_maximum_fusion.da_hbm, bf16[4,2,2,2,24,3072]{5,4,3,2,1,0:T(8,128)(2,1)} %bitcast.114, bf16[4,2,2,2,96,768]{5,4,3,2,1,0:T(8,128)(2,1)} %bitcast.113, ...), custom_call_target="tpu_custom_call" | custom-call | tf_op jit(solution)/shard_map/scatter_gradients/pallas_call | solution.py:685
  357.8 0.8 slice_reduce_fusion
  359.3 1.2 slice_bitcast_fusion.6
  360.6 0.5 multiply_convert_fusion.4
  361.3 1.5 slice_bitcast_fusion.3
  362.8 0.6 multiply_convert_fusion.2
  363.5 1.7 fusion.47
  365.2 4.2 %add_bitcast_fusion = f32[1,512,768]{2,1,0:T(8,128)} fusion(bf16[512,768]{1,0:T(8,128)(2,1)} %collective-permute-done, f32[1024,768]{1,0:T(8,128)} %convolution_add_fusion, s32[]{:T(128)S(6)} %select_n.54, bf16[512,768]{1,0:T(8,128)(2,1)S(1)} %copy-done.7, f32[512,768]{1,0:T(8,128)S(1)} %get-tuple-element.84, bf16[768,3072]{1,0:T(8,128)(2,1)} %bitcast.123, ...), kind=kOutput, calls=%fused_computation.43 | convolution fusion | flops 605945856 | bytes 7473156 | tf_op jit(solution)/shard_map/dot_general | solution.py:34
  369.4 0.9 copy.63
  370.3 0.7 copy.64
  371.0 0.7 copy.65
  (109 shorter events, 2.5 us)
Async XLA Ops:
  0.7 0.8 copy-start
  122.2 4.3 %copy-start.2 = (f32[512,768]{1,0:T(8,128)S(1)}, f32[512,768]{1,0:T(8,128)}, u32[]{:S(2)}) copy-start(f32[512,768]{1,0:T(8,128)} %get-tuple-element.46) | copy-start | bytes 4718596
  126.5 5.0 %copy-start.3 = (f32[512,768]{1,0:T(8,128)S(1)}, f32[512,768]{1,0:T(8,128)}, u32[]{:S(2)}) copy-start(f32[512,768]{1,0:T(8,128)} %get-tuple-element.50) | copy-start | bytes 4718596
  131.5 1.4 copy-start.4
  131.7 21.4 %slice-start = ((s8[4718592]{0:T(1024)(128)(4,1)}), s8[4194304]{0:T(1024)(128)(4,1)S(1)}, s32[]{:S(2)}) async-start(s8[4718592]{0:T(1024)(128)(4,1)} %bitcast.136), calls=%async_computation | async-start | bytes 8388608
  133.1 20.0 %copy-start.8 = (bf16[512,768]{1,0:T(8,128)(2,1)}, bf16[512,768]{1,0:T(8,128)(2,1)S(1)}, u32[]{:S(2)}) copy-start(bf16[512,768]{1,0:T(8,128)(2,1)S(1)} %get-tuple-element.80) | copy-start | bytes 2359300
  133.1 20.0 %slice-start.1 = ((s8[4718592]{0:T(1024)(128)(4,1)}), s8[524288]{0:T(1024)(128)(4,1)S(1)}, s32[]{:S(2)}) async-start(s8[4718592]{0:T(1024)(128)(4,1)} %bitcast.136), calls=%async_computation.1 | async-start | bytes 1048576
  153.1 3.2 copy-start.23
  157.2 0.9 copy-start.13
  202.6 162.6 %collective-permute-start = (bf16[512,768]{1,0:T(8,128)(2,1)}, bf16[512,768]{1,0:T(8,128)(2,1)}, u32[]{:S(2)}, u32[]{:S(2)}) collective-permute-start(bf16[512,768]{1,0:T(8,128)(2,1)} %dynamic-slice_convert_fusion), channel_id=1, source_target_pairs={{0,1},{1,0},{2,3},{3,2},{4,5},{5,4},{6,7},{7,6},{8,9},{9,8},{10,11... | collective-permute-start | bytes 2359304 | tf_op jit(solution)/shard_map/ppermute | solution.py:786
  208.4 4.5 %copy-start.5 = (bf16[1024,768]{1,0:T(8,128)(2,1)S(1)}, bf16[1024,768]{1,0:T(8,128)(2,1)}, u32[]{:S(2)}) copy-start(bf16[1024,768]{1,0:T(8,128)(2,1)} %get-tuple-element.58) | copy-start | bytes 4718596
  208.4 4.5 %copy-start.9 = (bf16[768,1024]{1,0:T(8,128)(2,1)S(1)}, bf16[768,1024]{1,0:T(8,128)(2,1)}, u32[]{:S(2)}) copy-start(bf16[768,1024]{1,0:T(8,128)(2,1)} %copy.55) | copy-start | bytes 4718596
  212.9 2.5 copy-start.6
  212.9 2.7 copy-start.11
  218.3 10.2 %copy-start.24 = (bf16[512,3072]{1,0:T(8,128)(2,1)S(1)}, bf16[512,3072]{1,0:T(8,128)(2,1)}, u32[]{:S(2)}) copy-start(bf16[512,3072]{1,0:T(8,128)(2,1)} %copy-done.23) | copy-start | bytes 9437188
  228.5 4.8 %copy-start.14 = (bf16[512,768]{1,0:T(8,128)(2,1)S(1)}, bf16[512,768]{1,0:T(8,128)(2,1)}, u32[]{:S(2)}) copy-start(bf16[512,768]{1,0:T(8,128)(2,1)} %copy-done.13) | copy-start | bytes 2359300
  228.5 4.8 %copy-start.21 = (bf16[512,768]{1,0:T(8,128)(2,1)S(1)}, bf16[512,768]{1,0:T(8,128)(2,1)}, u32[]{:S(2)}) copy-start(bf16[512,768]{1,0:T(8,128)(2,1)} %get-tuple-element.60) | copy-start | bytes 2359300
  233.3 1.8 copy-start.19
  233.3 2.0 copy-start.10
  242.8 117.8 %copy-start.22 = (bf16[24]{0:T(256)(128)(2,1)S(1)}, bf16[24]{0:T(256)(128)(2,1)}, u32[]{:S(2)}) copy-start(bf16[24]{0:T(256)(128)(2,1)} %param.23) | copy-start | bytes 148
  242.8 120.0 %copy-start.17 = (bf16[24,768]{1,0:T(8,128)(2,1)S(1)}, bf16[24,768]{1,0:T(8,128)(2,1)}, u32[]{:S(2)}) copy-start(bf16[24,768]{1,0:T(8,128)(2,1)} %wq.1) | copy-start | bytes 110596
  242.8 120.0 %copy-start.18 = (bf16[24,768]{1,0:T(8,128)(2,1)S(1)}, bf16[24,768]{1,0:T(8,128)(2,1)}, u32[]{:S(2)}) copy-start(bf16[24,768]{1,0:T(8,128)(2,1)} %wk.1) | copy-start | bytes 110596
  242.8 122.3 %copy-start.7 = (bf16[512,768]{1,0:T(8,128)(2,1)S(1)}, bf16[512,768]{1,0:T(8,128)(2,1)}, u32[]{:S(2)}) copy-start(bf16[512,768]{1,0:T(8,128)(2,1)} %get-tuple-element.56) | copy-start | bytes 2359300
  358.6 10.7 %copy-start.20 = (f32[12]{0:T(128)}, f32[12]{0:T(128)S(1)}, u32[]{:S(2)}) copy-start(f32[12]{0:T(128)S(1)} %slice_reduce_fusion) | copy-start | bytes 148
  365.2 4.2 %copy-start.12 = (bf16[512,768]{1,0:T(8,128)(2,1)S(1)}, bf16[512,768]{1,0:T(8,128)(2,1)}, u32[]{:S(2)}) copy-start(bf16[512,768]{1,0:T(8,128)(2,1)} %get-tuple-element.44) | copy-start | bytes 2359300
  365.2 5.1 %copy-start.16 = (f32[24,3072]{1,0:T(8,128)S(1)}, f32[24,3072]{1,0:T(8,128)}, u32[]{:S(2)}) copy-start(f32[24,3072]{1,0:T(8,128)} %get-tuple-element.149) | copy-start | bytes 884740
  365.2 5.8 %copy-start.15 = (f32[96,768]{1,0:T(8,128)S(1)}, f32[96,768]{1,0:T(8,128)}, u32[]{:S(2)}) copy-start(f32[96,768]{1,0:T(8,128)} %get-tuple-element.151) | copy-start | bytes 884740
  365.2 6.5 %copy-start.1 = (s32[1,16,12,3]{1,0,3,2:T(1,128)S(1)}, s32[1,16,12,3]{1,0,3,2:T(1,128)}, u32[]{:S(2)}) copy-start(s32[1,16,12,3]{1,0,3,2:T(1,128)} %param.38) | copy-start | bytes 6916

commit v2 on v1

--- a/solution.py
+++ b/solution.py
@@ -96,10 +96,9 @@
 
 
 class Gather:
-    def __init__(self, remote, place, buf, width):
+    def __init__(self, remote, place, buf, lo, width):
         z, x, c, y = place.z, place.x, place.c, place.y
-        half = width // 2
-        a, b = slice(0, half), slice(half, width)
+        a, b, both = slice(lo, lo + width // 2), slice(lo + width // 2, lo + width), slice(lo, lo + width)
         zs = range(1, place.nz)
 
         def make(ref, peer):
@@ -111,8 +110,8 @@
         self.by = make(buf.at[z, x, c, y, :, b], place.at(y=1 - y))
         self.bz = [make(buf.at[z, x, c, :, :, b], place.at(z=place.z_off(k))) for k in zs]
         self.bx = make(buf.at[:, x, c, :, :, b], place.at(x=1 - x))
-        self.ca = make(buf.at[:, :, c, :, :, a], place.at(c=1 - c))
-        self.cb = make(buf.at[:, :, c, :, :, b], place.at(c=1 - c))
+        self.core = make(buf.at[:, :, c, :, :, both], place.at(c=1 - c))
+        self.steps = 5
 
     def step(self, n):
         if n == 0:
@@ -123,26 +122,57 @@
             self.by.wait_recv()
             for copy in self.bz:
                 copy.start()
-        elif n == 2:
             for copy in self.az:
                 copy.wait_recv()
             self.ax.start()
-        elif n == 3:
+        elif n == 2:
+            self.ax.wait_recv()
+            self.ay.start()
             for copy in self.bz:
                 copy.wait_recv()
             self.bx.start()
+        elif n == 3:
+            self.ay.wait_recv()
+            self.bx.wait_recv()
+            self.core.start()
         elif n == 4:
-            self.ax.wait_recv()
-            self.ay.start()
-        elif n == 5:
-            self.bx.wait_recv()
-            self.cb.start()
-        elif n == 6:
-            self.ay.wait_recv()
-            self.ca.start()
-        elif n == 7:
-            self.ca.wait_recv()
-            self.cb.wait_recv()
+            self.core.wait_recv()
+
+
+class SmallGather:
+    def __init__(self, remote, place, buf):
+        z, x, c, y = place.z, place.x, place.c, place.y
+        self.stages = [
+            [remote.make(buf.at[z, x, c, y], buf.at[z, x, c, y], place.at(z=place.z_off(k))) for k in range(1, place.nz)],
+            [remote.make(buf.at[:, x, c, y], buf.at[:, x, c, y], place.at(x=1 - x))],
+            [remote.make(buf.at[:, :, c, y], buf.at[:, :, c, y], place.at(y=1 - y))],
+            [remote.make(buf.at[:, :, c], buf.at[:, :, c], place.at(c=1 - c))],
+        ]
+        self.steps = 5
+
+    def step(self, n):
+        if n > 0:
+            for copy in self.stages[n - 1]:
+                copy.wait_recv()
+        if n < 4:
+            for copy in self.stages[n]:
+                copy.start()
+
+
+class Rounds:
+    def __init__(self):
+        self.active = []
+
+    def add(self, *items):
+        for item in items:
+            item.step(0)
+            self.active.append([item, 1])
+
+    def round(self):
+        for entry in self.active:
+            entry[0].step(entry[1])
+            entry[1] += 1
+        self.active = [e for e in self.active if e[1] < e[0].steps]
 
 
 def layer_norm_parts(rows):
@@ -186,24 +216,23 @@
 
 def forward_kernel(
     nz, local, length_ref, compact_ref, x_hbm, wq, wk, wv, wo, wi, wu, small,
-    out_hbm, r1_hbm, u_hbm, r2_hbm, a_hbm, q_hbm, k_hbm, v_hbm, xf_hbm, lse_hbm, top_hbm, wa_hbm, wi_hbm, wu_hbm, vec_hbm,
-    WA, WI, WU, SM, XF, Q, K, V, VT, AT, A, R1, R2, N1L, U, G, PB, S, E, VEC, IB, LSE, TOP, OUT,
+    out_hbm, r1_hbm, r2_hbm, gp_hbm, gt_hbm, n1t_hbm, at_hbm, q_hbm, k_hbm, kt_hbm, v_hbm, xt_hbm, lse_hbm, top_hbm,
+    wa_hbm, wi_hbm, wu_hbm, vec_hbm,
+    WA, WI, WU, SM, XF, XT, Q, K, KT, V, VT, AT, R1, R2, N1L, N1T, U, GP, G, GT, E, VEC, IB, LSE, TOP, OUT,
     send_sems, recv_sems, local_sems, out_sems,
 ):
     place = Place(nz)
     z, x, c, y = place.z, place.x, place.c, place.y
     remote = Remote(send_sems, recv_sems)
     mine = (z, x, c, y)
-    locals_ = [
-        pltpu.make_async_copy(x_hbm, XF.at[y], local_sems.at[0]),
-        pltpu.make_async_copy(wq, WA.at[(*mine, slice(None), slice(0, D))], local_sems.at[1]),
-        pltpu.make_async_copy(wk, WA.at[(*mine, slice(None), slice(D, 2 * D))], local_sems.at[2]),
-        pltpu.make_async_copy(wv, WA.at[(*mine, slice(None), slice(2 * D, 3 * D))], local_sems.at[3]),
-        pltpu.make_async_copy(wo, WA.at[(*mine, slice(None), slice(3 * D, 4 * D))], local_sems.at[4]),
-        pltpu.make_async_copy(wi, WI.at[mine], local_sems.at[5]),
-        pltpu.make_async_copy(wu, WU.at[mine], local_sems.at[6]),
-        pltpu.make_async_copy(small, SM.at[mine], local_sems.at[7]),
-    ]
+    seq_len = 2 * local
+    locals_ = [(x_hbm, XF.at[y]), (small, SM.at[mine])]
+    for g in range(3):
+        for n, w in enumerate((wq, wk, wv)):
+            lo = g * D + n * 256
+            locals_.append((w.at[:, g * 256 : (g + 1) * 256], WA.at[(*mine, slice(None), slice(lo, lo + 256))]))
+    locals_ += [(wo, WA.at[(*mine, slice(None), slice(3 * D, 4 * D))]), (wi, WI.at[mine]), (wu, WU.at[mine])]
+    locals_ = [pltpu.make_async_copy(src, dst, local_sems.at[k]) for k, (src, dst) in enumerate(locals_)]
     for copy in locals_:
         copy.start()
     entry_barrier(place)
@@ -217,72 +246,31 @@
         copy.start()
         outs.append(copy)
 
-    xs = remote.make(XF.at[y], XF.at[y], place.at(y=1 - y))
-    ga = Gather(remote, place, WA, 4 * D)
-    gi = Gather(remote, place, WI, FF)
-    gu = Gather(remote, place, WU, D)
-    sz = [remote.make(SM.at[mine], SM.at[mine], place.at(z=place.z_off(k))) for k in range(1, nz)]
-    sx = remote.make(SM.at[:, x, c, y], SM.at[:, x, c, y], place.at(x=1 - x))
-    sy = remote.make(SM.at[:, :, c, y], SM.at[:, :, c, y], place.at(y=1 - y))
-    sc = remote.make(SM.at[:, :, c], SM.at[:, :, c], place.at(c=1 - c))
-
-    ga.step(0)
-    for copy in sz:
-        copy.start()
+    other = 1 - y
+    xs = remote.make(XF.at[y], XF.at[y], place.at(y=other))
+    chunks = [Gather(remote, place, WA, g * D, D) for g in range(4)]
+    chunks += [Gather(remote, place, WI, n * D, D) for n in range(FF // D)]
+    chunks += [Gather(remote, place, WU, n * 256, 256) for n in range(3)]
+    rounds = Rounds()
+    rounds.add(chunks[0], SmallGather(remote, place, SM))
     xs.start()
     length = length_ref[0]
-    seq_len = XF.shape[0] * local
     E[...] = key_structure(seq_len, length)
-    ga.step(1)
-    ga.step(2)
-    for copy in sz:
-        copy.wait_recv()
-    sx.start()
-    ga.step(3)
-    ga.step(4)
-    sx.wait_recv()
-    sy.start()
-    gi.step(0)
-    gu.step(0)
-    ga.step(5)
-    ga.step(6)
-    sy.wait_recv()
-    sc.start()
-    sc.wait_recv()
-    ga.step(7)
-    gi.step(1)
-    gu.step(1)
-    gi.step(2)
-    put(WA, wa_hbm)
+    for n in range(1, 4):
+        rounds.round()
+        rounds.add(chunks[n])
+    own_rows = pl.ds(pl.multiple_of(y * local, local), local)
+    other_rows = pl.ds(pl.multiple_of(other * local, local), local)
+    XT[:, own_rows] = XF[y].T
+    rounds.round()
+    rounds.add(chunks[4])
+    xs.wait_recv()
 
     tiles = SM[...].reshape(-1, 16, 128)
     pieces = tiles.shape[0]
     VEC[...] = spread_vectors(tiles, D // pieces, pieces)
     IB[...] = spread_vectors(tiles[:, 8:16, :], FF // pieces, pieces)
     put(VEC, vec_hbm)
-
-    def wa(which):
-        return WA[:, :, :, :, :, which * D : (which + 1) * D].reshape(D, D)
-
-    Q[...] = ((dot_nn(XF[y], wa(0)) + VEC[0:1, :]).astype(bf16).astype(f32) * (HD**-0.5)).astype(bf16)
-    put(Q, q_hbm)
-    gu.step(2)
-    gi.step(3)
-    xs.wait_recv()
-    put(XF, xf_hbm)
-    for part in range(XF.shape[0]):
-        rows = slice(part * local, (part + 1) * local)
-        K[rows, :] = dot_nn(XF[part], wa(1)).astype(bf16)
-    gu.step(3)
-    gi.step(4)
-    for part in range(XF.shape[0]):
-        rows = slice(part * local, (part + 1) * local)
-        values = (dot_nn(XF[part], wa(2)) + VEC[1:2, :]).astype(bf16)
-        V[rows, :] = values
-        VT[:, rows] = values.T
-    put(K, k_hbm)
-    put(V, v_hbm)
-
     position = y * local + lax.broadcasted_iota(jnp.int32, (1, local), 1)
     live = position < length
 
@@ -303,35 +291,40 @@
             AT[own, cols] = dot_nn(VT[own, :], low).astype(bf16)
             LSE[h, :, cols] = top + jnp.log(total)
             TOP[h, :, cols] = jnp.where(live[:, cols], top, neg_large)
-
-        @pl.when(h == 0)
-        def _():
-            gu.step(4)
-
-        @pl.when(h == 1)
-        def _():
-            gi.step(5)
-
-        @pl.when(h == 2)
-        def _():
-            gu.step(5)
-
-        @pl.when(h == 4)
-        def _():
-            gi.step(6)
-
-        @pl.when(h == 6)
-        def _():
-            gu.step(6)
-
         return carry
 
-    lax.fori_loop(0, H, head_step, 0)
+    def wide(buf, lo, width):
+        return buf[:, :, :, :, :, lo : lo + width].reshape(-1, width)
+
+    for g in range(3):
+        cols = slice(g * 256, (g + 1) * 256)
+        lo = g * D
+        own = dot_nn(XF[y], wide(WA, lo, D))
+        Q[:, cols] = ((own[:, :256] + VEC[0:1, cols]).astype(bf16).astype(f32) * (HD**-0.5)).astype(bf16)
+        K[own_rows, cols] = own[:, 256:512].astype(bf16)
+        values = (own[:, 512:] + VEC[1:2, cols]).astype(bf16)
+        V[own_rows, cols] = values
+        VT[cols, own_rows] = values.T
+        theirs = dot_nn(XF[other], wide(WA, lo + 256, 512))
+        K[other_rows, cols] = theirs[:, :256].astype(bf16)
+        values = (theirs[:, 256:] + VEC[1:2, cols]).astype(bf16)
+        V[other_rows, cols] = values
+        VT[cols, other_rows] = values.T
+        lax.fori_loop(4 * g, 4 * g + 2, head_step, 0)
+        rounds.round()
+        rounds.add(chunks[5 + 2 * g])
+        lax.fori_loop(4 * g + 2, 4 * g + 4, head_step, 0)
+        if g < 2:
+            rounds.round()
+            rounds.add(chunks[6 + 2 * g])
+    put(WA, wa_hbm)
+    put(Q, q_hbm)
+    put(K, k_hbm)
+    put(V, v_hbm)
     put(LSE, lse_hbm)
     put(TOP, top_hbm)
-    A[...] = AT[...].T
-    put(A, a_hbm)
-    R1[...] = dot_nn(A[...], wa(3))
+    put(AT, at_hbm)
+    R1[...] = dot_nn(AT[...].T, wide(WA, 3 * D, D))
 
     def first_norm(k, carry):
         rows = ds128(k, 64)
@@ -345,21 +338,34 @@
 
     lax.fori_loop(0, local // 64, first_norm, 0)
     put(R1, r1_hbm)
-    gi.step(7)
+    rounds.round()
+    rounds.add(chunks[10])
+    N1T[...] = N1L[...].T
+    put(N1T, n1t_hbm)
+    KT[...] = K[...].T
+    put(KT, kt_hbm)
+    XT[:, other_rows] = XF[other].T
+    put(XT, xt_hbm)
+    for n in range(FF // D):
+        cols = slice(n * D, (n + 1) * D)
+        U[...] = dot_nn(N1L[...], wide(WI, n * D, D)) + IB[0:1, cols]
+
+        def activate(k, carry):
+            rows = ds128(k, 16)
+            u = U[rows, :]
+            below = 0.5 * (1.0 + lax.erf(u * np.float32(0.5**0.5)))
+            G[rows, cols] = (u * below).astype(bf16)
+            GP[n, rows, :] = below + u * jnp.exp(-0.5 * u * u) * np.float32((2.0 * np.pi) ** -0.5)
+            return carry
+
+        lax.fori_loop(0, local // 16, activate, 0)
+        GT[cols, :] = G[:, cols].T
+        rounds.round()
     put(WI, wi_hbm)
-    for part in range(3):
-        cols = slice(part * 1024, (part + 1) * 1024)
-        U[:, cols] = dot_nn(N1L[...], WI[:, :, :, :, :, cols].reshape(D, 1024)) + IB[0:1, cols]
-
-    def activate(k, carry):
-        rows = ds128(k, 16)
-        u = U[rows, :]
-        G[rows, :] = (u * (0.5 * (1.0 + lax.erf(u * np.float32(0.5**0.5))))).astype(bf16)
-        return carry
-
-    lax.fori_loop(0, local // 16, activate, 0)
-    put(U, u_hbm)
-    gu.step(7)
+    put(GP, gp_hbm)
+    put(GT, gt_hbm)
+    while rounds.active:
+        rounds.round()
     put(WU, wu_hbm)
     R2[...] += dot_nn(G[...], WU[...].reshape(FF, D))
 
@@ -383,20 +389,21 @@
     grid = (nz, 2, 2, 2)
     rows, rows_u = wq.shape[0], wu.shape[0]
     seq = 2 * local
+    blocks = FF // D
     outs = [
-        ((local, D), bf16), ((local, D), f32), ((local, FF), f32), ((local, D), f32), ((local, D), bf16),
-        ((local, D), bf16), ((seq, D), bf16), ((seq, D), bf16), ((2, local, D), bf16),
-        ((H, 1, local), f32), ((H, 1, local), f32),
+        ((local, D), bf16), ((local, D), f32), ((local, D), f32), ((blocks, local, D), f32), ((FF, local), bf16),
+        ((D, local), bf16), ((D, local), bf16), ((local, D), bf16), ((seq, D), bf16), ((D, seq), bf16), ((seq, D), bf16),
+        ((D, seq), bf16), ((H, 1, local), f32), ((H, 1, local), f32),
         ((*grid, rows, 4 * D), bf16), ((*grid, rows, FF), bf16), ((*grid, rows_u, D), bf16), ((16, D), f32),
     ]
     scratch = [
         ((*grid, rows, 4 * D), bf16), ((*grid, rows, FF), bf16), ((*grid, rows_u, D), bf16), ((*grid, 16, 128), bf16),
-        ((2, local, D), bf16), ((local, D), bf16), ((seq, D), bf16), ((seq, D), bf16), ((D, seq), bf16),
-        ((D, local), bf16), ((local, D), bf16), ((local, D), f32), ((local, D), f32), ((local, D), bf16),
-        ((local, FF), f32), ((local, FF), bf16), ((8, 128), bf16), ((8, 128), f32), ((seq, 128), bf16),
+        ((2, local, D), bf16), ((D, seq), bf16), ((local, D), bf16), ((seq, D), bf16), ((D, seq), bf16), ((seq, D), bf16),
+        ((D, seq), bf16), ((D, local), bf16), ((local, D), f32), ((local, D), f32), ((local, D), bf16), ((D, local), bf16),
+        ((local, D), f32), ((blocks, local, D), f32), ((local, FF), bf16), ((FF, local), bf16), ((seq, 128), bf16),
         ((16, D), f32), ((8, FF), f32), ((H, 1, local), f32), ((H, 1, local), f32), ((local, D), bf16),
     ]
-    copies = 1 + 3 * (2 * (nz - 1) + 6) + (nz - 1) + 3
+    copies = 1 + 11 * (2 * (nz - 1) + 5) + (nz - 1) + 3
     return pl.pallas_call(
         functools.partial(forward_kernel, nz, local),
         out_shape=[jax.ShapeDtypeStruct(*o) for o in outs],
@@ -406,7 +413,7 @@
         + [
             pltpu.SemaphoreType.DMA((copies,)),
             pltpu.SemaphoreType.DMA((copies,)),
-            pltpu.SemaphoreType.DMA((8,)),
+            pltpu.SemaphoreType.DMA((14,)),
             pltpu.SemaphoreType.DMA((len(outs),)),
         ],
         compiler_params=pltpu.CompilerParams(collective_id=1, has_side_effects=True, vmem_limit_bytes=60 << 20),
@@ -433,7 +440,7 @@
     return jnp.stack(rows)
 
 
-def back_pair(pair, local, compact_ref, Q, K, V, KT, DA, LSE, E, PB, DS, DQT, DK, DV):
+def back_pair(pair, local, compact_ref, Q, K, V, KT, DA, LSE, E, PB, DS, DQT, DKG, DVG):
     lanes = ds128(pair, 128)
     q_pair, a_pair, k_pair, v_pair = Q[:, lanes], DA[:, lanes], K[:, lanes], V[:, lanes]
     left = jnp.concatenate([k_pair, E[...]], axis=1)
@@ -453,45 +460,19 @@
             low = (prob * (dprob - inner)).astype(bf16)
             DS[:, place] = low
             DQT[own, cols] = (dot_nn(KT[own, :], low) * (HD**-0.5)).astype(bf16)
-    DK[:, lanes] = dot_nn(DS[...], jnp.concatenate(q_heads, axis=0)).astype(bf16)
-    DV[:, lanes] = dot_nn(PB[...], jnp.concatenate(a_heads, axis=0)).astype(bf16)
-
-
-def attend_back_kernel(local, length_ref, compact_ref, Q, K, V, DA, LSE, DQ, DK, DV, E, KT, PB, DS, DQT):
-    E[...] = key_structure(K.shape[0], length_ref[0])
-    KT[...] = K[...].T
-
-    def step(pair, carry):
-        back_pair(pair, local, compact_ref, Q, K, V, KT, DA, LSE, E, PB, DS, DQT, DK, DV)
-        return carry
-
-    lax.fori_loop(0, H // 2, step, 0)
-    DQ[...] = DQT[...].T
-
-
-def run_attend_back(q, k, v, da, lse, compact, length):
-    local, seq = q.shape[0], k.shape[0]
-    outs = [((local, D), bf16), ((seq, D), bf16), ((seq, D), bf16)]
-    scratch = [((seq, 128), bf16), ((D, seq), bf16), ((seq, 2 * local), bf16), ((seq, 2 * local), bf16), ((D, local), bf16)]
-    return pl.pallas_call(
-        functools.partial(attend_back_kernel, local),
-        out_shape=[jax.ShapeDtypeStruct(*o) for o in outs],
-        in_specs=[INSMEM] + [INVMEM] * 6,
-        out_specs=[INVMEM] * 3,
-        scratch_shapes=[pltpu.VMEM(*s) for s in scratch],
-        compiler_params=pltpu.CompilerParams(vmem_limit_bytes=60 << 20),
-        name="attend_back",
-    )(length, compact, q, k, v, da, lse)
+    spot = ds128(lax.rem(pair, 2), 128)
+    DKG[:, spot] = dot_nn(DS[...], jnp.concatenate(q_heads, axis=0)).astype(bf16)
+    DVG[:, spot] = dot_nn(PB[...], jnp.concatenate(a_heads, axis=0)).astype(bf16)
 
 
 class Scatter:
-    def __init__(self, remote, place, g, bufs, out, width):
+    def __init__(self, remote, place, g, bufs, out, lo, width):
         rc, ra1, ra2, raz, rb1, rbz, rb2 = bufs
         z, x, c, y = place.z, place.x, place.c, place.y
         half = width // 2
-        a, b = slice(0, half), slice(half, width)
-        self.place, self.g, self.bufs, self.out, self.a, self.b = place, g, bufs, out, a, b
-        self.core = remote.make(g.at[:, :, 1 - c], rc, place.at(c=1 - c))
+        a, b, both = slice(lo, lo + half), slice(lo + half, lo + width), slice(lo, lo + width)
+        self.place, self.g, self.bufs, self.out, self.a, self.b, self.both = place, g, bufs, out, a, b, both
+        self.core = remote.make(g.at[:, :, 1 - c, :, :, both], rc, place.at(c=1 - c))
         self.a1 = remote.make(g.at[:, :, c, 1 - y, :, a], ra1, place.at(y=1 - y))
         self.b1 = remote.make(g.at[:, 1 - x, c, :, :, b], rb1, place.at(x=1 - x))
         self.a2 = remote.make(g.at[:, 1 - x, c, y, :, a], ra2, place.at(x=1 - x))
@@ -501,10 +482,11 @@
             self.bz.append(remote.make(g.at[zk, x, c, :, :, b], rbz.at[k - 1], place.at(z=zk)))
             self.az.append(remote.make(g.at[zk, x, c, y, :, a], raz.at[k - 1], place.at(z=zk)))
         self.b2 = remote.make(g.at[z, x, c, 1 - y, :, b], rb2, place.at(y=1 - y))
+        self.steps = 5
 
     def step(self, n):
         rc, ra1, ra2, raz, rb1, rbz, rb2 = self.bufs
-        place, g, a, b = self.place, self.g, self.a, self.b
+        place, g, a, b, both = self.place, self.g, self.a, self.b, self.both
         z, x, c, y = place.z, place.x, place.c, place.y
         if n == 0:
             self.core.start()
@@ -514,13 +496,24 @@
             def add_core(k, carry):
                 zz, xx = lax.div(k, 2), lax.rem(k, 2)
                 for yy in range(2):
-                    g[zz, xx, c, yy] = (g[zz, xx, c, yy].astype(f32) + rc[zz, xx, yy].astype(f32)).astype(bf16)
+                    total = g[zz, xx, c, yy, :, both].astype(f32) + rc[zz, xx, yy].astype(f32)
+                    g[zz, xx, c, yy, :, both] = total.astype(bf16)
                 return carry
 
             lax.fori_loop(0, place.nz * 2, add_core, 0)
             self.a1.start()
             self.b1.start()
         elif n == 2:
+            self.b1.wait_recv()
+
+            def add_b1(k, carry):
+                zz, yy = lax.div(k, 2), lax.rem(k, 2)
+                g[zz, x, c, yy, :, b] = (g[zz, x, c, yy, :, b].astype(f32) + rb1[zz, yy].astype(f32)).astype(bf16)
+                return carry
+
+            lax.fori_loop(0, place.nz * 2, add_b1, 0)
+            for copy in self.bz:
+                copy.start()
             self.a1.wait_recv()
 
             def add_a1(k, carry):
@@ -531,39 +524,34 @@
             lax.fori_loop(0, place.nz * 2, add_a1, 0)
             self.a2.start()
         elif n == 3:
-            self.b1.wait_recv()
-
-            def add_b1(k, carry):
-                zz, yy = lax.div(k, 2), lax.rem(k, 2)
-                g[zz, x, c, yy, :, b] = (g[zz, x, c, yy, :, b].astype(f32) + rb1[zz, yy].astype(f32)).astype(bf16)
+            self.a2.wait_recv()
+
+            def add_a2(zz, carry):
+                g[zz, x, c, y, :, a] = (g[zz, x, c, y, :, a].astype(f32) + ra2[zz].astype(f32)).astype(bf16)
                 return carry
 
-            lax.fori_loop(0, place.nz * 2, add_b1, 0)
-            for copy in self.bz:
-                copy.start()
-        elif n == 4:
-            self.a2.wait_recv()
-            for zz in range(place.nz):
-                g[zz, x, c, y, :, a] = (g[zz, x, c, y, :, a].astype(f32) + ra2[zz].astype(f32)).astype(bf16)
+            lax.fori_loop(0, place.nz, add_a2, 0)
             for copy in self.az:
                 copy.start()
-        elif n == 5:
             for copy in self.bz:
                 copy.wait_recv()
-            for yy in range(2):
+
+            def add_bz(yy, carry):
                 total = g[z, x, c, yy, :, b].astype(f32)
                 for k in range(place.nz - 1):
                     total = total + rbz[k, yy].astype(f32)
                 g[z, x, c, yy, :, b] = total.astype(bf16)
+                return carry
+
+            lax.fori_loop(0, 2, add_bz, 0)
             self.b2.start()
-        elif n == 6:
+        elif n == 4:
             for copy in self.az:
                 copy.wait_recv()
             total = g[z, x, c, y, :, a].astype(f32)
             for k in range(place.nz - 1):
                 total = total + raz[k].astype(f32)
             self.out[:, a] = total
-        elif n == 7:
             self.b2.wait_recv()
             self.out[:, b] = g[z, x, c, y, :, b].astype(f32) + rb2[...].astype(f32)
 
@@ -577,10 +565,10 @@
 
 
 class SmallSums:
-    def __init__(self, remote, place, t, bufs, top, tops):
+    def __init__(self, remote, place, t, bufs):
         rc, ry, rx, rz = bufs
         z, x, c, y = place.z, place.x, place.c, place.y
-        self.place, self.t, self.bufs, self.top, self.tops = place, t, bufs, top, tops
+        self.place, self.t, self.bufs = place, t, bufs
         self.stages = [
             [remote.make(t.at[:, :, 1 - c], rc, place.at(c=1 - c))],
             [remote.make(t.at[:, :, c, 1 - y], ry, place.at(y=1 - y))],
@@ -590,108 +578,320 @@
                 for k in range(1, place.nz)
             ],
         ]
+        self.steps = 5
+
+    def step(self, n):
+        place, t = self.place, self.t
+        rc, ry, rx, rz = self.bufs
+        z, x, c, y = place.z, place.x, place.c, place.y
+        if n > 0:
+            for copy in self.stages[n - 1]:
+                copy.wait_recv()
+        if n == 1:
+            t[:, :, c] = t[:, :, c] + rc[...]
+        elif n == 2:
+            t[:, :, c, y] = t[:, :, c, y] + ry[...]
+        elif n == 3:
+            t[:, x, c, y] = t[:, x, c, y] + rx[...]
+        elif n == 4:
+            total = t[z, x, c, y]
+            for k in range(place.nz - 1):
+                total = total + rz[k]
+            t[z, x, c, y] = total
+        if n < 4:
+            for copy in self.stages[n]:
+                copy.start()
+
+
+def small_buffers(nz):
+    return [((nz, 2, 2, 16, 128), f32), ((nz, 2, 16, 128), f32), ((nz, 16, 128), f32), ((nz - 1, 16, 128), f32)]
+
+
+class TopOfAll:
+    def __init__(self, remote, place, top, tops):
+        x, c, y = place.x, place.c, place.y
         to = [[place.at(c=1 - c)], [place.at(y=1 - y)], [place.at(x=1 - x)]]
         to.append([place.at(z=place.z_off(k)) for k in range(1, place.nz)])
-        self.top_stages, slot = [], 0
+        self.top, self.tops, self.stages, slot = top, tops, [], 0
         for n, peers in enumerate(to):
             made = []
             for peer in peers:
                 made.append((remote.make(top.at[n], tops.at[slot], peer), slot))
                 slot += 1
-            self.top_stages.append(made)
-
-    def start(self, n):
-        for copy in self.stages[n]:
-            copy.start()
-        for copy, _ in self.top_stages[n]:
-            copy.start()
-
-    def take(self, n):
-        place, t = self.place, self.t
-        rc, ry, rx, rz = self.bufs
-        z, x, c, y = place.z, place.x, place.c, place.y
-        for copy in self.stages[n]:
-            copy.wait_recv()
-        best = self.top[n]
-        for copy, slot in self.top_stages[n]:
-            copy.wait_recv()
-            best = jnp.maximum(best, self.tops[slot])
-        self.top[n + 1] = best
-        if n == 0:
-            t[:, :, c] = t[:, :, c] + rc[...]
-        elif n == 1:
-            t[:, :, c, y] = t[:, :, c, y] + ry[...]
-        elif n == 2:
-            t[:, x, c, y] = t[:, x, c, y] + rx[...]
-        else:
-            total = t[z, x, c, y]
-            for k in range(place.nz - 1):
-                total = total + rz[k]
-            t[z, x, c, y] = total
-
-
-def small_buffers(nz):
-    return [((nz, 2, 2, 16, 128), f32), ((nz, 2, 16, 128), f32), ((nz, 16, 128), f32), ((nz - 1, 16, 128), f32)]
-
-
-def scatter_kernel(nz, widths, da_hbm, di_hbm, du_hbm, sm_hbm, top_hbm, oa, oi, ou, osm, otop, *rest):
+            self.stages.append(made)
+        self.steps = 5
+
+    def step(self, n):
+        if n > 0:
+            best = self.top[n - 1]
+            for copy, slot in self.stages[n - 1]:
+                copy.wait_recv()
+                best = jnp.maximum(best, self.tops[slot])
+            self.top[n] = best
+        if n < 4:
+            for copy, _ in self.stages[n]:
+                copy.start()
+
+
+def gather_vectors(rows, width, pieces):
+    n, total = rows.shape
+    lane3 = lax.broadcasted_iota(jnp.int32, (pieces, n, total), 2).astype(f32)
+    piece3 = lax.broadcasted_iota(jnp.int32, (pieces, n, total), 0).astype(f32)
+    mine = jnp.floor((lane3 + 0.5) * (1.0 / width)) == piece3
+    spread = jnp.where(mine, rows[None], 0.0).reshape(pieces * n, total)
+    lane = lax.broadcasted_iota(jnp.int32, (128, total), 1).astype(f32)
+    row = lax.broadcasted_iota(jnp.int32, (128, total), 0).astype(f32)
+    owner = jnp.floor((lane + 0.5) * (1.0 / width))
+    chooser = jnp.where(lane - owner * width == row, 1.0, 0.0).astype(bf16)
+    high = spread.astype(bf16)
+    rest = spread - high.astype(f32)
+    middle = rest.astype(bf16)
+    lowest = (rest - middle.astype(f32)).astype(bf16)
+    tiles = dot_nt(high, chooser) + (dot_nt(middle, chooser) + dot_nt(lowest, chooser))
+    return tiles.reshape(pieces, n, 128)
+
+
+def norm_back(normal, inverse, grads, gain):
+    scaled = grads * gain
+    first = jnp.mean(scaled, axis=-1, keepdims=True)
+    second = jnp.mean(scaled * normal, axis=-1, keepdims=True)
+    return inverse * (scaled - first - normal * second)
+
+
+def row_sum(values):
+    return jnp.sum(values, axis=0, keepdims=True)
+
+
+def backward_kernel(
+    nz, local, length_ref, compact_ref, VEC, cot_hbm, r1_hbm, r2_hbm, gp_hbm, gt_hbm, n1t_hbm, at_hbm, q_hbm, k_hbm, kt_hbm,
+    v_hbm, xt_hbm, lse_hbm, top_hbm, wa_hbm, wi_hbm, wu_hbm,
+    dx_hbm, OA, OI, OU, OS, OT, *rest,
+):
     place = Place(nz)
-    ga, gi, gu, t, top, tops = rest[:6]
-    bufs = [rest[6 + 7 * k : 13 + 7 * k] for k in range(3)]
-    sbufs = rest[27:31]
-    send_sems, recv_sems, local_sems = rest[31:]
-    loads = [
-        pltpu.make_async_copy(src, dst, local_sems.at[k])
-        for k, (src, dst) in enumerate([(sm_hbm, t), (top_hbm, top.at[0]), (du_hbm, gu), (di_hbm, gi), (da_hbm, ga)])
+    z, x, c, y = place.z, place.x, place.c, place.y
+    GA, GI, GU, WA, T, TOP, TOPS, TOPV, DP, DA, AT, DR1, E, SUMS, ISUM, SEND, RECV = rest[:17]
+    bufs = [rest[17 + 7 * k : 24 + 7 * k] for k in range(11)]
+    sbufs = rest[94:98]
+    send_sems, recv_sems, load_sems = rest[98:]
+    blocks = FF // D
+    pieces = nz * 8
+    seq_len = 2 * local
+    length = length_ref[0]
+    loads = [0]
+
+    def load(src, dst):
+        copy = pltpu.make_async_copy(src, dst, load_sems.at[loads[0]])
+        loads[0] += 1
+        copy.start()
+        return copy
+
+    remote = Remote(send_sems, recv_sems)
+    ups = [Scatter(remote, place, GU, bufs[n], OU, n * 256, 256) for n in range(3)]
+    ins = [Scatter(remote, place, GI, bufs[3 + n], OI, n * D, D) for n in range(blocks)]
+    att = [Scatter(remote, place, GA, bufs[7 + n], OA, n * D, D) for n in range(4)]
+    small = SmallSums(remote, place, T, sbufs)
+    best = TopOfAll(remote, place, TOP, TOPS)
+    swap = remote.make(SEND, RECV, place.at(y=1 - y))
+    rounds = Rounds()
+    grid = (nz, 2, 2, 2)
+    SUMS[...] = jnp.zeros_like(SUMS)
+    ISUM[...] = jnp.zeros_like(ISUM)
+
+    def first_stage(COT, R2, R1, DM, GT, DU, GP, N1T, WUS, WIS):
+        l_r2, l_cot = load(r2_hbm, R2), load(cot_hbm, COT)
+        l_wu = [load(wu_hbm.at[0], WUS.at[0]), load(wu_hbm.at[1], WUS.at[1])]
+        l_gp = [load(gp_hbm.at[0], GP.at[0]), load(gp_hbm.at[1], GP.at[1])]
+        l_gt = load(gt_hbm, GT)
+        l_n1t, l_r1 = load(n1t_hbm, N1T), load(r1_hbm, R1)
+
+        def wi_of(n):
+            return wi_hbm.at[:, :, :, :, :, n * D : (n + 1) * D]
+
+        l_wi = [load(wi_of(0), WIS.at[0]), load(wi_of(1), WIS.at[1])]
+        l_top, l_at, l_wa = load(top_hbm, TOPV), load(at_hbm, AT), load(wa_hbm, WA)
+        entry_barrier(place)
+        E[...] = key_structure(seq_len, length)
+        l_r2.wait()
+        l_cot.wait()
+
+        def second_norm(k, carry):
+            rows = ds128(k, 64)
+            normal, inverse = layer_norm_parts(R2[rows, :])
+            position = y * local + k * 64 + lax.broadcasted_iota(jnp.int32, (64, D), 0)
+            grads = jnp.where(position < length, COT[rows, :].astype(f32), 0.0)
+            through = norm_back(normal, inverse, grads, VEC[6:7, :])
+            R2[rows, :] = through
+            low = through.astype(bf16)
+            DM[rows, :] = low
+            SUMS[5:6, :] += row_sum(low.astype(f32))
+            SUMS[6:7, :] += row_sum(grads * normal)
+            SUMS[7:8, :] += row_sum(grads)
+            return carry
+
+        lax.fori_loop(0, local // 64, second_norm, 0)
+        for n in range(blocks):
+            l_wu[n].wait()
+            l_gp[n].wait()
+            grads = dot_nt(DM[...], WUS[n % 2].reshape(D, D)) * GP[n % 2]
+            low = grads.astype(bf16)
+            DU[n] = low
+            ISUM[0:1, n * D : (n + 1) * D] = row_sum(low.astype(f32))
+            if n + 2 < blocks:
+                l_wu.append(load(wu_hbm.at[n + 2], WUS.at[n % 2]))
+                l_gp.append(load(gp_hbm.at[n + 2], GP.at[n % 2]))
+        l_gt.wait()
+        for n in range(3):
+            cols = slice(n * 256, (n + 1) * 256)
+
+            def outer_grad(zz, carry):
+                rows = ds128(zz, FF // nz)
+                made = dot_nn(GT[rows, :], DM[:, cols]).astype(bf16)
+                GU[zz, :, :, :, :, cols] = made.reshape(2, 2, 2, -1, 256)
+                return carry
+
+            lax.fori_loop(0, nz, outer_grad, 0)
+            rounds.round()
+            rounds.add(ups[n])
+        l_top.wait()
+        TOP[0] = jnp.zeros((16, 128), f32) + neg_large
+        TOP[0, 0:H, :] = jnp.broadcast_to(jnp.max(TOPV[:, 0, :], axis=1, keepdims=True), (H, 128))
+        l_n1t.wait()
+        for n in range(blocks):
+            made = dot_nn(N1T[...], DU[n]).astype(bf16)
+            GI[:, :, :, :, :, n * D : (n + 1) * D] = made.reshape(*grid, -1, D)
+            rounds.round()
+            rounds.add(ins[n])
+            if n == 0:
+                rounds.add(best)
+        for n in range(blocks):
+            l_wi[n].wait()
+            R2[...] += dot_nt(DU[n], WIS[n % 2].reshape(D, D))
+            if n + 2 < blocks:
+                l_wi.append(load(wi_of(n + 2), WIS.at[n % 2]))
+        rounds.round()
+        l_r1.wait()
+
+        def first_norm(k, carry):
+            rows = ds128(k, 64)
+            normal, inverse = layer_norm_parts(R1[rows, :])
+            grads = R2[rows, :]
+            through = norm_back(normal, inverse, grads, VEC[3:4, :])
+            DR1[rows, :] = through
+            low = through.astype(bf16)
+            DP[rows, :] = low
+            SUMS[2:3, :] += row_sum(low.astype(f32))
+            SUMS[3:4, :] += row_sum(grads * normal)
+            SUMS[4:5, :] += row_sum(grads)
+            return carry
+
+        lax.fori_loop(0, local // 64, first_norm, 0)
+        l_at.wait()
+        l_wa.wait()
+
+    pl.run_scoped(
+        first_stage,
+        pltpu.VMEM((local, D), bf16), pltpu.VMEM((local, D), f32), pltpu.VMEM((local, D), f32), pltpu.VMEM((local, D), bf16),
+        pltpu.VMEM((FF, local), bf16), pltpu.VMEM((blocks, local, D), bf16), pltpu.VMEM((2, local, D), f32),
+        pltpu.VMEM((D, local), bf16), pltpu.VMEM((2, 2, 2, 2, FF // (nz * 8), D), bf16),
+        pltpu.VMEM((2, *grid, D // (nz * 8), D), bf16),
+    )
+
+    def second_stage(Q, K, KT, V, XT, LSE, PB, DS, DQT, DKG, DVG, DX, DXO):
+        waits = [load(s, d) for s, d in ((q_hbm, Q), (k_hbm, K), (kt_hbm, KT), (v_hbm, V), (lse_hbm, LSE), (xt_hbm, XT))]
+        made = dot_nn(AT[...], DP[...]).astype(bf16)
+        GA[:, :, :, :, :, 3 * D : 4 * D] = made.reshape(*grid, -1, D)
+        rounds.round()
+        rounds.add(att[3])
+        DA[...] = dot_nt(DP[...], WA[:, :, :, :, :, 3 * D : 4 * D].reshape(D, D)).astype(bf16)
+        for wait in waits:
+            wait.wait()
+        DX[...] = jnp.zeros_like(DX)
+        DXO[...] = jnp.zeros_like(DXO)
+        own_rows = pl.ds(pl.multiple_of(y * local, local), local)
+        other_rows = pl.ds(pl.multiple_of((1 - y) * local, local), local)
+
+        def pair_step(pair, carry):
+            back_pair(pair, local, compact_ref, Q, K, V, KT, DA, LSE, E, PB, DS, DQT, DKG, DVG)
+            return carry
+
+        for g in range(3):
+            lo = g * D
+            cols = slice(g * 256, (g + 1) * 256)
+            lax.fori_loop(2 * g, 2 * g + 1, pair_step, 0)
+            rounds.round()
+            lax.fori_loop(2 * g + 1, 2 * g + 2, pair_step, 0)
+            dq = DQT[cols, :].T
+            SUMS[0:1, cols] = row_sum(dq.astype(f32))
+            SUMS[1:2, cols] = row_sum(DVG[...].astype(f32))
+            for n, made in enumerate((dot_nn(XT[:, own_rows], dq), dot_nn(XT[...], DKG[...]), dot_nn(XT[...], DVG[...]))):
+                GA[:, :, :, :, :, lo + n * 256 : lo + (n + 1) * 256] = made.astype(bf16).reshape(*grid, -1, 256)
+            rounds.round()
+            rounds.add(att[g])
+            theirs = jnp.concatenate([DKG[other_rows, :], DVG[other_rows, :]], axis=1)
+            DXO[...] += dot_nt(theirs, WA[:, :, :, :, :, lo + 256 : lo + D].reshape(D, 512))
+            if g == 2:
+                SEND[...] = DXO[...].astype(bf16)
+                swap.start()
+            ours = jnp.concatenate([dq, DKG[own_rows, :], DVG[own_rows, :]], axis=1)
+            DX[...] += dot_nt(ours, WA[:, :, :, :, :, lo : lo + D].reshape(D, D))
+        rounds.round()
+        T[:, :, :, :, 0:8, :] = gather_vectors(SUMS[0:8, :], D // pieces, pieces).reshape(*grid, 8, 128)
+        wide = gather_vectors(ISUM[...], FF // pieces, pieces)
+        T[:, :, :, :, 8:16, :] = wide.reshape(*grid, 8, 128)
+        rounds.add(small)
+        while rounds.active:
+            rounds.round()
+        swap.wait_recv()
+
+        def last(k, carry):
+            rows = ds128(k, 64)
+            DX[rows, :] = DX[rows, :] + DR1[rows, :] + RECV[rows, :].astype(f32)
+            return carry
+
+        lax.fori_loop(0, local // 64, last, 0)
+        out = pltpu.make_async_copy(DX, dx_hbm, load_sems.at[loads[0]])
+        out.start()
+        OS[...] = T[z, x, c, y]
+        OT[...] = TOP[4]
+        out.wait()
+
+    pl.run_scoped(
+        second_stage,
+        pltpu.VMEM((local, D), bf16), pltpu.VMEM((seq_len, D), bf16), pltpu.VMEM((D, seq_len), bf16),
+        pltpu.VMEM((seq_len, D), bf16), pltpu.VMEM((D, seq_len), bf16), pltpu.VMEM((H, 1, local), f32),
+        pltpu.VMEM((seq_len, 2 * local), bf16), pltpu.VMEM((seq_len, 2 * local), bf16), pltpu.VMEM((D, local), bf16),
+        pltpu.VMEM((seq_len, 256), bf16), pltpu.VMEM((seq_len, 256), bf16), pltpu.VMEM((local, D), f32),
+        pltpu.VMEM((local, D), f32),
+    )
+    remote.finish()
+
+
+def run_backward(nz, local, rows, rows_u, length, compact, vec, *arrays):
+    grid = (nz, 2, 2, 2)
+    seq = 2 * local
+    outs = [((local, D), f32), ((rows, 4 * D), f32), ((rows, FF), f32), ((rows_u, D), f32), ((16, 128), f32), ((16, 128), f32)]
+    scratch = [
+        ((*grid, rows, 4 * D), bf16), ((*grid, rows, FF), bf16), ((*grid, rows_u, D), bf16), ((*grid, rows, 4 * D), bf16),
+        ((*grid, 16, 128), f32), ((5, 16, 128), f32), ((3 + nz - 1, 16, 128), f32), ((H, 1, local), f32),
+        ((local, D), bf16), ((local, D), bf16), ((D, local), bf16), ((local, D), f32), ((seq, 128), bf16),
+        ((8, D), f32), ((8, FF), f32), ((local, D), bf16), ((local, D), bf16),
     ]
-    for copy in loads:
-        copy.start()
-    entry_barrier(place)
-    remote = Remote(send_sems, recv_sems)
-    small = SmallSums(remote, place, t, sbufs, top, tops)
-    parts = [
-        Scatter(remote, place, g, bufs[k], out, width)
-        for k, (g, out, width) in enumerate([(gu, ou, widths[2]), (gi, oi, widths[1]), (ga, oa, widths[0])])
-    ]
-    loads[0].wait()
-    loads[1].wait()
-    small.start(0)
-    for n, part in enumerate(parts):
-        loads[2 + n].wait()
-        part.step(0)
-    small.take(0)
-    small.start(1)
-    for n in range(1, 8):
-        for part in parts:
-            part.step(n)
-        if n < 4:
-            small.take(n)
-            if n < 3:
-                small.start(n + 1)
-    osm[...] = t[place.z, place.x, place.c, place.y]
-    otop[...] = top[4]
-    remote.finish()
-
-
-def run_scatter(nz, da, di, du, sm, top):
-    grid = (nz, 2, 2, 2)
-    shapes = [a.shape[-2:] for a in (da, di, du)]
-    outs = [(s, f32) for s in shapes] + [((16, 128), f32), ((16, 128), f32)]
-    scratch = [(a.shape, bf16) for a in (da, di, du)] + [(sm.shape, f32), ((5, 16, 128), f32), ((3 + nz - 1, 16, 128), f32)]
-    for s in (shapes[2], shapes[1], shapes[0]):
-        scratch += scatter_buffers(nz, *s)
+    for n in range(3):
+        scratch += scatter_buffers(nz, rows_u, 256)
+    for n in range(8):
+        scratch += scatter_buffers(nz, rows, D)
     scratch += small_buffers(nz)
-    copies = 3 * (2 * (nz - 1) + 5) + 2 * (3 + nz - 1)
+    copies = 11 * (2 * (nz - 1) + 5) + 2 * (3 + nz - 1) + 1
     return pl.pallas_call(
-        functools.partial(scatter_kernel, nz, [s[1] for s in shapes]),
+        functools.partial(backward_kernel, nz, local),
         out_shape=[jax.ShapeDtypeStruct(*o) for o in outs],
-        in_specs=[ANY] * 5,
-        out_specs=[INVMEM] * 5,
+        in_specs=[INSMEM, INVMEM, INVMEM] + [ANY] * len(arrays),
+        out_specs=[ANY] + [INVMEM] * 5,
         scratch_shapes=[pltpu.VMEM(*s) for s in scratch]
-        + [pltpu.SemaphoreType.DMA((copies,)), pltpu.SemaphoreType.DMA((copies,)), pltpu.SemaphoreType.DMA((5,))],
+        + [pltpu.SemaphoreType.DMA((copies,)), pltpu.SemaphoreType.DMA((copies,)), pltpu.SemaphoreType.DMA((32,))],
         compiler_params=pltpu.CompilerParams(collective_id=2, has_side_effects=True, vmem_limit_bytes=60 << 20),
-        name="scatter_gradients",
-    )(da, di, du, sm, top)
+        name="backward_scatter",
+    )(length, compact, vec, *arrays)
 
 
 def layer_norm(row_values, gain_vector, shift_vector):
@@ -720,13 +920,6 @@
     return query_clipped, (query_bias.astype(f32) * bias_scale).astype(bf16), key_clipped
 
 
-def tiles_of(vectors, wide, pieces, grid):
-    rows = [jnp.pad(v.reshape(pieces, -1), ((0, 0), (0, 128 - v.shape[0] // pieces))) for v in vectors]
-    rows.append(jnp.pad(wide.reshape(pieces, -1), ((0, 0), (0, 128 - wide.shape[0] // pieces))))
-    rows += [jnp.zeros((pieces, 128), f32)] * (16 - len(rows))
-    return jnp.stack(rows, axis=1).reshape(*grid, 16, 128)
-
-
 def fast_shards(
     nz,
     inputs, cotangent, query_weight, query_bias, key_weight, value_weight, value_bias, output_weight, output_bias,
@@ -734,7 +927,6 @@
     lengths, random_blocks, threshold,
 ):
     local = inputs.shape[1]
-    grid = (nz, 2, 2, 2)
     pieces = nz * 8
     rows, rows_u = query_weight.shape[0], outer_weight.shape[0]
     y = lax.axis_index("ctx")
@@ -748,63 +940,22 @@
     x = inputs[0]
     weights = (query_weight, key_weight, value_weight, output_weight, inner_weight, outer_weight)
     (
-        output, first_sum, pre_act, second_sum, attended, q, k, v, x_both, lse, tops, wa, wi, wu, vectors
+        output, r1, r2, gp, gt, n1t, at, q, k, kt, v, xt, lse, tops, wa, wi, wu, vectors
     ) = run_forward(nz, x, weights, small, compact, lengths)
-    wa, wi, wu = wa.reshape(D, 4 * D), wi.reshape(D, FF), wu.reshape(FF, D)
-    full_query, full_key, full_value, full_out = (wa[:, n * D : (n + 1) * D] for n in range(4))
-    gain_one, shift_one, gain_two, shift_two = vectors[3], vectors[4], vectors[6], vectors[7]
-    normed_low = layer_norm(first_sum, gain_one, shift_one).astype(bf16)
-    activated = gelu_exact(pre_act).astype(bf16)
-    live = (y * local + jnp.arange(local)) < lengths[0]
-    cot_rows = jnp.where(live[:, None], cotangent[0].astype(f32), 0.0)
-    second_pull = jax.vjp(layer_norm, second_sum, gain_two, shift_two)[1]
-    grad_second, second_gain_grad, second_shift_grad = second_pull(cot_rows)
-    grad_outer_low = grad_second.astype(bf16)
-    outer_bias_grad = column_sums(grad_outer_low)
-    outer_weight_grad = dot_tn(activated, grad_outer_low)
-    grad_activated = dot_nt(grad_outer_low, wu)
-    grad_pre_low = jax.vjp(gelu_exact, pre_act)[1](grad_activated)[0].astype(bf16)
-    inner_bias_grad = column_sums(grad_pre_low)
-    inner_weight_grad = dot_tn(normed_low, grad_pre_low)
-    grad_normed = grad_second + dot_nt(grad_pre_low, wi)
-    first_pull = jax.vjp(layer_norm, first_sum, gain_one, shift_one)[1]
-    grad_first, first_gain_grad, first_shift_grad = first_pull(grad_normed)
-    grad_proj_low = grad_first.astype(bf16)
-    output_bias_grad = column_sums(grad_proj_low)
-    output_weight_grad = dot_tn(attended, grad_proj_low)
-    grad_attended = dot_nt(grad_proj_low, full_out).astype(bf16)
-    dq, dk, dv = run_attend_back(q, k, v, grad_attended, lse, compact, lengths)
-    x_rows = x_both.reshape(2 * local, D)
-    query_weight_grad = dot_tn(x, dq)
-    query_bias_grad = column_sums(dq)
-    key_weight_grad = dot_tn(x_rows, dk)
-    value_weight_grad = dot_tn(x_rows, dv)
-    value_bias_grad = column_sums(dv)
-    through = dot_nt(dk, full_key) + dot_nt(dv, full_value)
-    own = lax.dynamic_slice_in_dim(through, y * local, local, 0)
-    other = lax.dynamic_slice_in_dim(through, (1 - y) * local, local, 0).astype(bf16)
-    received = lax.ppermute(other, "ctx", [(0, 1), (1, 0)]).astype(f32)
-    input_grad = grad_first + dot_nt(dq, full_query) + own + received
-    da = jnp.concatenate(
-        [query_weight_grad, key_weight_grad, value_weight_grad, output_weight_grad], axis=1
-    ).astype(bf16).reshape(*grid, rows, 4 * D)
-    di = inner_weight_grad.astype(bf16).reshape(*grid, rows, FF)
-    du = outer_weight_grad.astype(bf16).reshape(*grid, rows_u, D)
-    sm = tiles_of(
-        [query_bias_grad, value_bias_grad, output_bias_grad, first_gain_grad, first_shift_grad, outer_bias_grad,
-         second_gain_grad, second_shift_grad], inner_bias_grad, pieces, grid,
+    input_grad, ga, gi, gu, gs, top = run_backward(
+        nz, local, rows, rows_u, lengths, compact, vectors, cotangent[0], r1, r2, gp, gt, n1t, at, q, k, kt, v, xt, lse, tops,
+        wa, wi, wu,
     )
-    top_here = jnp.broadcast_to(jnp.pad(jnp.max(tops[:, 0, :], axis=1), (0, 4))[:, None], (16, 128))
-    ga, gi, gu, gs, top = run_scatter(nz, da, di, du, sm, top_here)
     logit_maxima = top[:H, 0]
     rank = lax.axis_index("dp") * 2 + y
     query_clipped, bias_clipped, key_clipped = clip_outputs(
         logit_maxima, threshold, query_weight, query_bias, key_weight, rank
     )
     vec = [gs[n, :rows] for n in range(8)]
+    qkv = [jnp.concatenate([ga[:, g * D + n * 256 : g * D + (n + 1) * 256] for g in range(3)], axis=1) for n in range(3)]
     return (
         output[None], input_grad[None],
-        ga[:, :D], vec[0], ga[:, D : 2 * D], ga[:, 2 * D : 3 * D], vec[1], ga[:, 3 * D :], vec[2], vec[3], vec[4],
+        qkv[0], vec[0], qkv[1], qkv[2], vec[1], ga[:, 3 * D :], vec[2], vec[3], vec[4],
         gi, gs[8, : FF // pieces], gu, vec[5], vec[6], vec[7],
         query_clipped, bias_clipped, key_clipped, logit_maxima,
     )

time: 376 us -> 267 us (0.71)
  matrix products: 66.8 us -> 0 us
  other arithmetic: 19.2 us -> 4.03 us
  Pallas kernels: 258 us -> 243 us
  local copies, waits for them, and re-layouts: 23.5 us -> 14.7 us
    dot_general x12 -> x0, matrix products: 66.8 us -> none  [the longest x6 41.1 us: dot_nt(): lax.dot_general(a, b, (((1,), (1,)), ((), ())), preferred_element_type=f32)]
    reduce_sum x11 -> x0, other arithmetic: 11.7 us -> none  [the longest x4 5.42 us: layer_norm(): centre = row_values - jnp.mean(row_values, axis=-1, keepdims=True)]
    pallas_call x2 -> x1, Pallas kernels: 143 us -> 133 us  [run_backward(): pl.pallas_call(functools.partial(backward_kernel, nz, local), out_shape=[...]
    pallas_call x1, Pallas kernels: 115 us -> 110 us  [run_forward(): pl.pallas_call(functools.partial(forward_kernel, nz, local), out_shape=[j...]
  transfers between devices with their start and end apart: 1 -> 0, of which waited for: 0 -> 0; matrix products, arithmetic and copies ran while one was open for 12% -> 0% of each run, Pallas kernels for 31% -> 0%
where the time goes in v2:
time: 267 us; the launch traced here: 264 us
  Pallas kernels  243 us (91%)
  local copies, waits for them, and re-layouts  14.7 us (6%)
  other arithmetic  4.03 us (2%)
    pallas_call x1, Pallas kernels, run_backward(): pl.pallas_call(functools.partial(backward_kernel, nz, local), out_shape=[...  133 us
    pallas_call x1, Pallas kernels, run_forward(): pl.pallas_call(functools.partial(forward_kernel, nz, local), out_shape=[j...  110 us

profile of v2, /device:TPU:0, one launch (start us, length us, event | category | flops | bytes accessed | tf_op | source)
XLA Modules:
  0.0 264.1 jit_solution(4477395588014813719)
XLA Ops:
  0.7 0.0 copy-start
  2.0 0.7 pad_bitcast_fusion.8
  2.7 0.1 fusion.6
  2.8 0.7 pad_bitcast_fusion.6
  3.5 0.7 pad_bitcast_fusion.4
  4.2 0.7 pad_bitcast_fusion
  4.8 0.7 pad_bitcast_fusion.2
  5.5 1.2 stack.47.small
  6.7 0.0 copy-done
  6.7 0.1 constant_dynamic-slice_fusion
  6.8 0.1 copy.49
  6.9 0.1 copy.50
  7.0 0.1 copy.52
  7.1 0.1 copy.51
  7.2 0.7 select_select_fusion.compact_ref
  7.9 110.3 %gather_forward.1 = (bf16[512,768]{1,0:T(8,128)(2,1)}, f32[512,768]{1,0:T(8,128)}, f32[512,768]{1,0:T(8,128)}, f32[4,512,768]{2,1,0:T(8,128)}, bf16[3072,512]{1,...) custom-call(s32[1]{0:T(128)S(6)} %copy.57.length_ref, ...), custom_call_target="tpu_custom_call" | custom-call | tf_op jit(solution)/shard_map/gather_forward/pallas_call | solution.py:407
  118.2 0.0 copy-start.8
  118.2 0.0 copy-start.5
  118.2 0.0 copy-start.6
  118.3 0.0 copy-start.2
  118.3 132.8 %backward_scatter.1 = (f32[512,768]{1,0:T(8,128)}, f32[24,3072]{1,0:T(8,128)}, f32[24,3072]{1,0:T(8,128)}, f32[96,768]{1,0:T(8,128)}, f32[16,128]{1,0:T(8,128)}, /*index=5*/f32[16,128]{1,0:T(8,128)}) custom-call(s32[1]{0:T(128)S(6)} %copy.57.length_ref, f32[12,8,128]{2,1,0:T(8,128)} %select_select_fusion.compact_ref, f32[16,768]{1,0:T(8,128)} %get-tuple-element.46.VEC, ...), custom_call_target="tpu_custom_call" | custom-call | tf_op jit(solution)/shard_map/backward_scatter/pallas_call | solution.py:885
  251.1 0.0 copy-start.1
  251.1 0.9 slice_reduce_fusion
  252.0 0.0 copy-start.7
  252.0 0.1 select_reduce_fusion
  252.1 0.0 copy-done.8
  252.1 0.5 multiply_convert_fusion.2
  252.7 1.2 slice_bitcast_fusion.6
  253.8 1.5 slice_bitcast_fusion.3
  255.3 0.1 broadcast_in_dim.66
  255.4 0.1 mul.37
  255.5 0.0 copy-done.5
  255.5 0.0 copy-done.6
  255.5 0.6 multiply_convert_fusion
  256.1 1.5 slice.83
  257.7 0.9 fusion.7
  258.6 0.6 pad_maximum_fusion.2
  259.2 0.6 pad_maximum_fusion.1
  259.8 0.6 pad_maximum_fusion
  260.5 0.0 copy-done.2
  260.5 0.9 copy.59
  261.4 0.0 copy-done.1
  261.4 1.1 copy.60
  262.5 0.0 copy-done.7
  262.5 0.0 copy-done.4
  262.5 0.7 copy.61
  263.2 0.0 copy-done.3
  263.2 0.7 copy.62
  (13 shorter events, 0.1 us)
Async XLA Ops:
  0.7 6.1 %copy-start = (s32[1,16,12,3]{1,0,3,2:T(1,128)S(1)}, s32[1,16,12,3]{1,0,3,2:T(1,128)}, u32[]{:S(2)}) copy-start(s32[1,16,12,3]{1,0,3,2:T(1,128)} %param.38) | copy-start | bytes 6916
  118.2 133.9 %copy-start.8 = (bf16[24]{0:T(256)(128)(2,1)S(1)}, bf16[24]{0:T(256)(128)(2,1)}, u32[]{:S(2)}) copy-start(bf16[24]{0:T(256)(128)(2,1)} %param.23) | copy-start | bytes 148
  118.2 137.3 %copy-start.5 = (bf16[24,768]{1,0:T(8,128)(2,1)S(1)}, bf16[24,768]{1,0:T(8,128)(2,1)}, u32[]{:S(2)}) copy-start(bf16[24,768]{1,0:T(8,128)(2,1)} %wq.1) | copy-start | bytes 110596
  118.2 137.3 %copy-start.6 = (bf16[24,768]{1,0:T(8,128)(2,1)S(1)}, bf16[24,768]{1,0:T(8,128)(2,1)}, u32[]{:S(2)}) copy-start(bf16[24,768]{1,0:T(8,128)(2,1)} %wk.1) | copy-start | bytes 110596
  118.3 142.2 %copy-start.2 = (bf16[512,768]{1,0:T(8,128)(2,1)S(1)}, bf16[512,768]{1,0:T(8,128)(2,1)}, u32[]{:S(2)}) copy-start(bf16[512,768]{1,0:T(8,128)(2,1)} %get-tuple-element.45) | copy-start | bytes 2359300
  251.1 10.3 %copy-start.1 = (f32[512,768]{1,0:T(8,128)S(1)}, f32[512,768]{1,0:T(8,128)}, u32[]{:S(2)}) copy-start(f32[512,768]{1,0:T(8,128)} %get-tuple-element.63) | copy-start | bytes 4718596
  252.0 10.5 %copy-start.7 = (f32[12]{0:T(128)}, f32[12]{0:T(128)S(1)}, u32[]{:S(2)}) copy-start(f32[12]{0:T(128)S(1)} %slice_reduce_fusion) | copy-start | bytes 148
  261.4 1.2 copy-start.4
  261.4 1.9 copy-start.3
